TPU v7x, 128 devices: a whole 4x4x4 slice. The times are simulated.
128 devices in a mesh: row: 8 (over x_hi, y), col: 16 (over z, x_lo, core).
Axes of the slice: x: 4 (x_hi: 2, x_lo: 2; x = x_hi * 2 + x_lo), y: 4, z: 4, core: 2. Of those that a mesh axis runs over, the one named last changes fastest.
Arguments:
- latent: bfloat16 [16, 524288], P(None, ('row', 'col')), may hold values from -200 to 200, as said below
- in_weight: bfloat16 [3, 3, 16, 512], replicated, may hold values from -0.5 to 0.5
- in_bias: float32 [512], replicated, may hold values from -3 to 3
- norm_gain: float32 [512], replicated, may hold values from 0.25 to 1.75
- norm_shift: float32 [512], replicated, may hold values from -3 to 3
- mid_weight: bfloat16 [512, 3, 3, 512], replicated, may hold values from -0.09375 to 0.09375
- mid_bias: float32 [512], replicated, may hold values from -3 to 3
Outputs:
- features: bfloat16 [512, 1024, 512], P('row', 'col')
Inputs may be any that keep to these rules, and one draw needn't show every extreme that they name: real-valued latent entries.
All inputs are finite; a program needn't handle non-finite values.
Results may differ from a plain program's by a relative error of at most 0.0095.
Values may be sent and summed in bfloat16 or wider, within the bound.
No kernel may reach another device: no remote copies, remote signals or barrier semaphores. Data moves between devices by JAX's collectives and lax.ppermute only.
A program may use at most 192 MiB of HBM per device.

v0:
```python
import functools

import jax
import jax.numpy as jnp
from jax import lax
from jax.experimental import pallas as pl
from jax.experimental.pallas import tpu as pltpu
from jax.sharding import PartitionSpec as P

C_LAT = 16
CH = 512
GROUPS = 32
TILE = 64
WIDTH = 1024
N_ROW = 8
N_COL = 16
N_DEV = N_ROW * N_COL
OWN = 4
ACT = TILE + 2
LAT = TILE + 4
PLANES = 6
EPSILON = 1e-06
BF16 = jnp.bfloat16
F32 = jnp.float32
VMEM = pl.BlockSpec(memory_space=pltpu.VMEM)
SMEM = pl.BlockSpec(memory_space=pltpu.SMEM)
MIB = 1 << 20


def dot_tn(lhs, rhs):
    return lax.dot_general(lhs, rhs, (((0,), (0,)), ((), ())), preferred_element_type=F32)


def dot_nt(lhs, rhs):
    return lax.dot_general(lhs, rhs, (((1,), (1,)), ((), ())), preferred_element_type=F32)


def pack_kernel(own, top, bot, out, rows):
    rows[0:16] = top[:, 0:WIDTH]
    rows[16:32] = top[:, WIDTH:]
    for r in range(OWN):
        rows[32 + 16 * r : 48 + 16 * r] = own[:, WIDTH * r : WIDTH * (r + 1)]
    rows[96:112] = bot[:, 0:WIDTH]
    rows[112:128] = bot[:, WIDTH:]
    k = lax.broadcasted_iota(jnp.int32, (384, 256), 0)
    n = lax.broadcasted_iota(jnp.int32, (384, 256), 1)
    lane = n % 128
    column = 64 * (n // 128) + 4 * (lane % 16) + lane // 16 + 126
    pick = jnp.where(k == column, 1.0, 0.0).astype(BF16)
    zero = jnp.zeros((128, 128), BF16)
    for t in range(8):
        parts = [
            rows[:, 128 * u : 128 * (u + 1)] if 0 <= u < 8 else zero for u in (t - 1, t, t + 1)
        ]
        moved = jnp.dot(jnp.concatenate(parts, axis=1), pick, preferred_element_type=F32)
        out[2 * t] = moved[:, :128].astype(BF16)
        out[2 * t + 1] = moved[:, 128:].astype(BF16)


def stats_kernel(own, top, bot, weight, bias, out, taps):
    column = lax.broadcasted_iota(jnp.int32, (C_LAT, WIDTH), 1)
    for r in range(OWN + 2):
        if r == 0:
            row = top[:, WIDTH:]
        elif r == OWN + 1:
            row = bot[:, 0:WIDTH]
        else:
            row = own[:, WIDTH * (r - 1) : WIDTH * r]
        wide = row.astype(F32)
        left = jnp.where(column == 0, 0.0, pltpu.roll(wide, 1, 1))
        right = jnp.where(column == WIDTH - 1, 0.0, pltpu.roll(wide, WIDTH - 1, 1))
        at = slice(16 * r, 16 * r + 16)
        taps[0, at] = left.astype(BF16)
        taps[1, at] = row
        taps[2, at] = right.astype(BF16)
    total = jnp.zeros((8, CH), F32)
    squares = jnp.zeros((8, CH), F32)
    for r in range(OWN):
        for half in range(2):
            cols = slice(512 * half, 512 * half + 512)
            patch = jnp.concatenate([taps[b, 16 * r : 16 * r + 48, cols] for b in range(3)], axis=0)
            value = (dot_tn(patch, weight[...]) + bias[...]).reshape(64, 8, CH)
            total = total + jnp.sum(value, axis=0)
            squares = squares + jnp.sum(value * value, axis=0)
    channel = lax.broadcasted_iota(jnp.int32, (CH, 128), 0) // (CH // GROUPS)
    lane = lax.broadcasted_iota(jnp.int32, (CH, 128), 1)
    to_sum = jnp.where(channel == lane, 1.0, 0.0)
    to_squares = jnp.where(channel == lane - GROUPS, 1.0, 0.0)
    both = jnp.dot(
        total, to_sum, precision=lax.Precision.HIGHEST, preferred_element_type=F32
    ) + jnp.dot(squares, to_squares, precision=lax.Precision.HIGHEST, preferred_element_type=F32)
    out[...] = jnp.broadcast_to(jnp.sum(both, axis=0).reshape(1, 1, 128), (N_DEV, 1, 128))


def affine(stats, bias, gain, shift):
    sums = jnp.sum(stats[...], axis=0)
    sums = jnp.broadcast_to(sums, (8, 128)) / (TILE * TILE * N_DEV * (CH // GROUPS))
    channel = lax.broadcasted_iota(jnp.int32, (128, CH), 1) // (CH // GROUPS)
    lane = lax.broadcasted_iota(jnp.int32, (128, CH), 0)
    spread = functools.partial(
        jnp.dot, precision=lax.Precision.HIGHEST, preferred_element_type=F32
    )
    mean = spread(sums, jnp.where(channel == lane, 1.0, 0.0))[0:1]
    square = spread(sums, jnp.where(channel == lane - GROUPS, 1.0, 0.0))[0:1]
    scale = lax.rsqrt(square - mean * mean + EPSILON) * gain[...]
    return scale, (bias[...] - mean) * scale + shift[...]


def main_kernel(
    place, recv, stats, in_weight, in_bias, gain, shift, weight, bias, out, lat, act, spread
):
    for s in range(N_COL):
        first, last = (0 if s == 0 else 32), (128 if s == N_COL - 1 else 96)
        rows = recv[s, first:last]
        wide = rows.astype(F32)
        at = pl.ds(64 * s + first, last - first)
        lat[0, at] = rows
        for b in (1, 2):
            lat[b, at] = pltpu.roll(wide, 128 - 16 * b, 1).astype(BF16)
    scale, offset = affine(stats, in_bias, gain, shift)
    half_scale, half_offset = 0.5 * scale, 0.5 * offset
    batch = 6

    def activate(step, _):
        row = step * batch
        patches = [
            jnp.concatenate(
                [lat[b, pl.ds(pl.multiple_of((row + j) * 16, 16), 48)] for b in range(3)], axis=0
            )
            for j in range(batch)
        ]
        value = dot_tn(jnp.concatenate(patches, axis=1), in_weight[...])
        for j in range(batch):
            half = value[128 * j : 128 * j + 96] * half_scale + half_offset
            act[row + j] = (half + half * jnp.tanh(half)).astype(BF16)
        return 0

    lax.fori_loop(0, ACT // batch, activate, 0)

    @pl.when(place[0] == 0)
    def _():
        act[0] = jnp.zeros((PLANES * 16, CH), BF16)

    @pl.when(place[0] == N_ROW - 1)
    def _():
        act[ACT - 1] = jnp.zeros((PLANES * 16, CH), BF16)

    cell = lax.broadcasted_iota(jnp.int32, (ACT, 16, CH), 1)

    @pl.when(place[1] == 0)
    def _():
        act[:, 0:16] = jnp.where(cell == 0, 0.0, act[:, 0:16].astype(F32)).astype(BF16)

    @pl.when(place[1] == N_COL - 1)
    def _():
        act[:, 80:96] = jnp.where(cell == 15, 0.0, act[:, 80:96].astype(F32)).astype(BF16)

    deep = 16

    def convolve(step, _):
        row = step * deep
        total = jnp.broadcast_to(bias[...], (deep * TILE, CH))
        for a in range(3):
            for b in range(3):
                cells = act[pl.ds(row + a, deep), 16 * b : 16 * b + 64].reshape(deep * TILE, CH)
                total = total + dot_nt(cells, weight[a, b])
        for r in range(deep):
            for t in range(4):
                at = 64 * r + 16 * t
                for l in range(4):
                    lanes = slice(128 * l, 128 * l + 128)
                    spread[r, l, pl.ds(t, 16, stride=4)] = total[at : at + 16, lanes]
        for r in range(deep):
            for l in range(4):
                out[row + r, :, 128 * l : 128 * l + 128] = spread[r, l].astype(BF16)
        return 0

    lax.fori_loop(0, TILE // deep, convolve, 0)


def body(latent, in_weight, in_bias, norm_gain, norm_shift, mid_weight, mid_bias):
    both = ("row", "col")
    up = [(i, i + 1) for i in range(N_DEV - 1)]
    down = [(i + 1, i) for i in range(N_DEV - 1)]
    top = lax.ppermute(latent[:, 2 * WIDTH :], both, up)
    bot = lax.ppermute(latent[:, : 2 * WIDTH], both, down)
    chunks = pl.pallas_call(
        pack_kernel,
        out_shape=jax.ShapeDtypeStruct((N_COL, 128, 128), BF16),
        in_specs=[VMEM] * 3,
        out_specs=VMEM,
        scratch_shapes=[pltpu.VMEM((128, WIDTH), BF16)],
        name="pack",
    )(latent, top, bot)
    recv = lax.all_to_all(chunks, "col", split_axis=0, concat_axis=0, tiled=True)
    taps = jnp.transpose(in_weight, (1, 0, 2, 3)).reshape(9 * C_LAT, CH)
    bias = in_bias.reshape(1, CH)
    partial = pl.pallas_call(
        stats_kernel,
        out_shape=jax.ShapeDtypeStruct((N_DEV, 1, 128), F32),
        in_specs=[VMEM] * 5,
        out_specs=VMEM,
        scratch_shapes=[pltpu.VMEM((3, 96, WIDTH), BF16)],
        name="stats",
    )(latent, top, bot, taps, bias)
    stats = lax.all_to_all(partial, both, split_axis=0, concat_axis=0, tiled=True)
    place = jnp.stack([lax.axis_index("row"), lax.axis_index("col")]).astype(jnp.int32)
    return pl.pallas_call(
        main_kernel,
        out_shape=jax.ShapeDtypeStruct((TILE, TILE, CH), BF16),
        in_specs=[SMEM] + [VMEM] * 8,
        out_specs=VMEM,
        scratch_shapes=[
            pltpu.VMEM((3, LAT * 16, 128), BF16),
            pltpu.VMEM((ACT, PLANES * 16, CH), BF16),
            pltpu.VMEM((16, 4, TILE, 128), F32),
        ],
        compiler_params=pltpu.CompilerParams(vmem_limit_bytes=48 * MIB),
        name="main",
    )(
        place,
        recv,
        stats,
        taps,
        bias,
        norm_gain.reshape(1, CH),
        norm_shift.reshape(1, CH),
        jnp.transpose(mid_weight, (1, 2, 0, 3)),
        mid_bias.reshape(1, CH),
    )


def solution(mesh):
    in_specs = (P(None, ("row", "col")), P(), P(), P(), P(), P(), P())
    return jax.shard_map(
        body, mesh=mesh, in_specs=in_specs, out_specs=P("row", "col", None), check_vma=False
    )
```

profile of v0, /device:TPU:1, one launch (start us, length us, event | category | flops | bytes accessed | tf_op | source)
XLA Modules:
  0.0 86.5 jit_solution(9742401147115323808)
XLA Ops:
  0.0 0.9 %fusion = (bf16[16,2048]{1,0:T(8,128)(2,1)S(1)}, bf16[16,2048]{1,0:T(8,128)(2,1)S(1)}) fusion(bf16[16,4096]{1,0:T(8,128)(2,1)} %own.3), kind=kLoop, calls=%fused_computation.1 | loop fusion | bytes 262144 | tf_op jit(solution)/shard_map/slice | solution.py:186
  0.9 3.3 %collective-permute-start.1 = (bf16[16,2048]{1,0:T(8,128)(2,1)S(1)}, bf16[16,2048]{1,0:T(8,128)(2,1)S(1)}, u32[]{:S(2)}, u32[]{:S(2)}) collective-permute-start(bf16[16,2048]{1,0:T(8,128)(2,1)S(1)} %get-tuple-element.5), channel_id=1, source_target_pairs={{1,0},{2,1},{3,2},{4,3},{5,4},{6,5},{7,6},{8,7},{9,8},{10,9},{11,1... | collective-permute-start | bytes 196616 | tf_op jit(solution)/shard_map/ppermute | solution.py:186
  4.2 3.1 %collective-permute-start = (bf16[16,2048]{1,0:T(8,128)(2,1)S(1)}, bf16[16,2048]{1,0:T(8,128)(2,1)S(1)}, u32[]{:S(2)}, u32[]{:S(2)}) collective-permute-start(bf16[16,2048]{1,0:T(8,128)(2,1)S(1)} %get-tuple-element.6), channel_id=1, source_target_pairs={{0,1},{1,2},{2,3},{3,4},{4,5},{5,6},{6,7},{7,8},{8,9},{9,10},{10,1... | collective-permute-start | bytes 196616 | tf_op jit(solution)/shard_map/ppermute | solution.py:185
  7.3 1.6 %copy.8 = bf16[3,3,16,512]{3,2,1,0:T(8,128)(2,1)} copy(bf16[3,3,16,512]{3,2,0,1:T(8,128)(2,1)} %bitcast.17) | data formatting | bytes 294912 | tf_op jit(solution)/shard_map/transpose | solution.py:196
  8.9 0.0 collective-permute-done.1.bot
  8.9 0.0 copy-start.6
  8.9 0.0 collective-permute-done.top
  8.9 0.0 copy-start.7
  8.9 0.6 copy-done.6
  9.5 0.0 copy-done.7
  9.6 4.1 %stats.1 = f32[128,1,128]{2,1,0:T(1,128)} custom-call(bf16[16,4096]{1,0:T(8,128)(2,1)} %own.3, bf16[16,2048]{1,0:T(8,128)(2,1)} %copy-done.7, bf16[16,2048]{1,0:T(8,128)(2,1)} %copy-done.6, bf16[144,512]{1,0:T(8,128)(2,1)} %bitcast.10, f32[1,512]{1,0:T(1,128)} %bitcast.12), custom_call_target="tpu_custom_call" | custom-call | tf_op jit(solution)/shard_map/stats/pallas_call | solution.py:198
  13.7 14.9 %all-to-all-start.1 = ((f32[128,1,128]{2,1,0:T(1,128)}), f32[128,1,128]{2,1,0:T(1,128)S(1)}, u32[]{:S(2)}, u32[]{:S(2)}) async-start(f32[128,1,128]{2,1,0:T(1,128)} %stats.1), calls=%async_computation.1 | async-start | bytes 131072 | tf_op jit(solution)/shard_map/all_to_all | solution.py:206
  28.6 2.2 %pack.1 = bf16[16,128,128]{2,1,0:T(8,128)(2,1)} custom-call(bf16[16,4096]{1,0:T(8,128)(2,1)} %own.3, bf16[16,2048]{1,0:T(8,128)(2,1)} %copy-done.7, bf16[16,2048]{1,0:T(8,128)(2,1)} %copy-done.6), custom_call_target="tpu_custom_call" | custom-call | tf_op jit(solution)/shard_map/pack/pallas_call | solution.py:187
  30.8 7.4 %all-to-all-done.1.stats = f32[128,1,128]{2,1,0:T(1,128)S(1)} async-done(((f32[128,1,128]{2,1,0:T(1,128)}), f32[128,1,128]{2,1,0:T(1,128)S(1)}, u32[]{:S(2)}, u32[]{:S(2)}) %all-to-all-start.1) | async-done | bytes 65568 | tf_op jit(solution)/shard_map/all_to_all | solution.py:206
  38.2 4.1 %all-to-all-start = ((bf16[16,128,128]{2,1,0:T(8,128)(2,1)}), bf16[16,128,128]{2,1,0:T(8,128)(2,1)S(1)}, u32[]{:S(2)}, u32[]{:S(2)}) async-start(bf16[16,128,128]{2,1,0:T(8,128)(2,1)} %pack.1), calls=%async_computation | async-start | bytes 1048576 | tf_op jit(solution)/shard_map/all_to_all | solution.py:195
  42.4 0.1 pad_add_fusion.place
  42.4 9.7 %all-to-all-done.recv = bf16[16,128,128]{2,1,0:T(8,128)(2,1)S(1)} async-done(((bf16[16,128,128]{2,1,0:T(8,128)(2,1)}), bf16[16,128,128]{2,1,0:T(8,128)(2,1)S(1)}, u32[]{:S(2)}, u32[]{:S(2)}) %all-to-all-start) | async-done | bytes 524320 | tf_op jit(solution)/shard_map/all_to_all | solution.py:195
  52.1 0.0 copy-start
  52.1 2.3 %copy-done = bf16[512,3,3,512]{3,0,2,1:T(8,128)(2,1)S(1)} copy-done((bf16[512,3,3,512]{3,0,2,1:T(8,128)(2,1)S(1)}, bf16[512,3,3,512]{3,0,2,1:T(8,128)(2,1)}, u32[]{:S(2)}) %copy-start) | copy-done | bytes 4718616
  54.5 0.0 copy-start.1
  54.5 0.9 %copy-done.1 = bf16[3,3,16,512]{3,2,1,0:T(8,128)(2,1)S(1)} copy-done((bf16[3,3,16,512]{3,2,1,0:T(8,128)(2,1)S(1)}, bf16[3,3,16,512]{3,2,1,0:T(8,128)(2,1)}, u32[]{:S(2)}) %copy-start.1) | copy-done | bytes 147480
  55.4 0.0 copy-start.2
  55.4 0.7 copy-done.2
  56.1 0.0 copy-start.3
  56.1 0.7 copy-done.3
  56.7 0.0 copy-start.4
  56.7 0.7 copy-done.4
  57.4 0.0 copy-start.5
  57.4 0.7 copy-done.5
  58.1 28.4 %main.1 = bf16[64,64,512]{2,1,0:T(8,128)(2,1)} custom-call(s32[2]{0:T(128)S(1)} %pad_add_fusion.place, bf16[16,128,128]{2,1,0:T(8,128)(2,1)S(1)} %all-to-all-done.recv, f32[128,1,128]{2,1,0:T(1,128)S(1)} %all-to-all-done.1.stats, bf16[144,512]{1,0:T(8,128)(2,1)S(1)} %bitcast.11, f32[1,512]{1,0:T(1,128)S(1)} %bitcast.13, f32[1,512]{1,0:T(1,128)S(1)} %bitcast.14, ...), custom_call_target="tpu_custom_call" | custom-call | tf_op jit(solution)/shard_map/main/pallas_call | solution.py:208
Async XLA Ops:
  0.9 8.0 %collective-permute-start.1 = (bf16[16,2048]{1,0:T(8,128)(2,1)S(1)}, bf16[16,2048]{1,0:T(8,128)(2,1)S(1)}, u32[]{:S(2)}, u32[]{:S(2)}) collective-permute-start(bf16[16,2048]{1,0:T(8,128)(2,1)S(1)} %get-tuple-element.5), channel_id=1, source_target_pairs={{1,0},{2,1},{3,2},{4,3},{5,4},{6,5},{7,6},{8,7},{9,8},{10,9},{11,1... | collective-permute-start | bytes 196616 | tf_op jit(solution)/shard_map/ppermute | solution.py:186
  4.2 4.7 %collective-permute-start = (bf16[16,2048]{1,0:T(8,128)(2,1)S(1)}, bf16[16,2048]{1,0:T(8,128)(2,1)S(1)}, u32[]{:S(2)}, u32[]{:S(2)}) collective-permute-start(bf16[16,2048]{1,0:T(8,128)(2,1)S(1)} %get-tuple-element.6), channel_id=1, source_target_pairs={{0,1},{1,2},{2,3},{3,4},{4,5},{5,6},{6,7},{7,8},{8,9},{9,10},{10,1... | collective-permute-start | bytes 196616 | tf_op jit(solution)/shard_map/ppermute | solution.py:185
  8.9 0.6 copy-start.6
  8.9 0.6 copy-start.7
  13.7 24.6 %all-to-all-start.1 = ((f32[128,1,128]{2,1,0:T(1,128)}), f32[128,1,128]{2,1,0:T(1,128)S(1)}, u32[]{:S(2)}, u32[]{:S(2)}) async-start(f32[128,1,128]{2,1,0:T(1,128)} %stats.1), calls=%async_computation.1 | async-start | bytes 131072 | tf_op jit(solution)/shard_map/all_to_all | solution.py:206
  38.2 13.9 %all-to-all-start = ((bf16[16,128,128]{2,1,0:T(8,128)(2,1)}), bf16[16,128,128]{2,1,0:T(8,128)(2,1)S(1)}, u32[]{:S(2)}, u32[]{:S(2)}) async-start(bf16[16,128,128]{2,1,0:T(8,128)(2,1)} %pack.1), calls=%async_computation | async-start | bytes 1048576 | tf_op jit(solution)/shard_map/all_to_all | solution.py:195
  52.1 2.3 %copy-start = (bf16[512,3,3,512]{3,0,2,1:T(8,128)(2,1)S(1)}, bf16[512,3,3,512]{3,0,2,1:T(8,128)(2,1)}, u32[]{:S(2)}) copy-start(bf16[512,3,3,512]{3,0,2,1:T(8,128)(2,1)} %param.12) | copy-start | bytes 14155780
  54.5 0.9 %copy-start.1 = (bf16[3,3,16,512]{3,2,1,0:T(8,128)(2,1)S(1)}, bf16[3,3,16,512]{3,2,1,0:T(8,128)(2,1)}, u32[]{:S(2)}) copy-start(bf16[3,3,16,512]{3,2,1,0:T(8,128)(2,1)} %copy.8) | copy-start | bytes 442372
  55.4 0.7 copy-start.2
  56.1 0.7 copy-start.3
  56.7 0.7 copy-start.4
  57.4 0.7 copy-start.5
where the time goes:
time: 87 us; the launch traced here: 86.5 us
  Pallas kernels  34.7 us (40%)
  starting transfers between devices  25.5 us (29%)
  waiting for transfers between devices  17.1 us (20%)
  local copies, waits for them, and re-layouts  9.07 us (10%)
    pallas_call x1, Pallas kernels, body(): pl.pallas_call(main_kernel, out_shape=jax.ShapeDtypeStruct((TILE, TILE, C...  28.4 us
    all_to_all x1, starting transfers between devices, body(): lax.all_to_all(partial, both, split_axis=0, concat_axis=0, tiled=True)  14.9 us
    all_to_all x1, waiting for transfers between devices, body(): lax.all_to_all(chunks, 'col', split_axis=0, concat_axis=0, tiled=True)  9.68 us
    all_to_all x1, waiting for transfers between devices, body(): lax.all_to_all(partial, both, split_axis=0, concat_axis=0, tiled=True)  7.39 us
    unnamed x16, local copies, waits for them, and re-layouts  6.61 us
    all_to_all x1, starting transfers between devices, body(): lax.all_to_all(chunks, 'col', split_axis=0, concat_axis=0, tiled=True)  4.13 us
    pallas_call x1, Pallas kernels, body(): pl.pallas_call(stats_kernel, out_shape=jax.ShapeDtypeStruct((N_DEV, 1, 12...  4.12 us
    ppermute x1, starting transfers between devices, body(): bot = lax.ppermute(latent[:, :2 * WIDTH], both, down)  3.29 us
  transfers between devices with their start and end apart: 4, of which 2 were waited for; matrix products, arithmetic and copies ran while one was open for 2% of the time, Pallas kernels for 3%

commit v1 on v0

v1 whole, which is shorter than its diff:
```python
import functools

import jax
import jax.numpy as jnp
from jax import lax
from jax.experimental import pallas as pl
from jax.experimental.pallas import tpu as pltpu
from jax.sharding import PartitionSpec as P

C_LAT = 16
CH = 512
GROUPS = 32
TILE = 64
WIDTH = 1024
N_ROW = 8
N_COL = 16
N_DEV = N_ROW * N_COL
OWN = 4
ACT = TILE + 2
LAT = TILE + 4
PLANES = 6
EPSILON = 1e-06
BF16 = jnp.bfloat16
F32 = jnp.float32
VMEM = pl.BlockSpec(memory_space=pltpu.VMEM)
SMEM = pl.BlockSpec(memory_space=pltpu.SMEM)
HBM = pl.BlockSpec(memory_space=pltpu.HBM)
MIB = 1 << 20


def dot_tn(lhs, rhs):
    return lax.dot_general(lhs, rhs, (((0,), (0,)), ((), ())), preferred_element_type=F32)


def dot_nt(lhs, rhs):
    return lax.dot_general(lhs, rhs, (((1,), (1,)), ((), ())), preferred_element_type=F32)


def hbm(array):
    return pltpu.with_memory_space_constraint(array, pltpu.HBM)


def start_copies(sources, targets, sems):
    copies = [
        pltpu.make_async_copy(source, target, sems.at[i])
        for i, (source, target) in enumerate(zip(sources, targets))
    ]
    for copy in copies:
        copy.start()
    return copies


def pack_kernel(place, own_hbm, top, bot, out, rows, own, sems):
    copies = start_copies((own_hbm,), (own,), sems)

    @pl.when(place[1] == 0)
    def _():
        rows[64:80] = top[:, 0:WIDTH]
        rows[80:96] = top[:, WIDTH:]

    @pl.when(place[1] != 0)
    def _():
        rows[64:80] = bot[:, 0:WIDTH]
        rows[80:96] = bot[:, WIDTH:]

    k = lax.broadcasted_iota(jnp.int32, (384, 256), 0)
    n = lax.broadcasted_iota(jnp.int32, (384, 256), 1)
    lane = n % 128
    column = 64 * (n // 128) + 4 * (lane % 16) + lane // 16 + 126
    pick = jnp.where(k == column, 1.0, 0.0).astype(BF16)
    zero = jnp.zeros((96, 128), BF16)
    copies[0].wait()
    for r in range(OWN):
        rows[16 * r : 16 * r + 16] = own[:, WIDTH * r : WIDTH * (r + 1)]
    for t in range(8):
        parts = [
            rows[:, 128 * u : 128 * (u + 1)] if 0 <= u < 8 else zero for u in (t - 1, t, t + 1)
        ]
        moved = jnp.dot(jnp.concatenate(parts, axis=1), pick, preferred_element_type=F32)
        out[2 * t] = moved[:, :128].astype(BF16)
        out[2 * t + 1] = moved[:, 128:].astype(BF16)


def stats_kernel(own_hbm, top, bot, weight_hbm, bias_hbm, out, taps, own, weight, bias, sems):
    copies = start_copies((own_hbm, weight_hbm, bias_hbm), (own, weight, bias), sems)
    copies[0].wait()
    column = lax.broadcasted_iota(jnp.int32, (C_LAT, WIDTH), 1)
    for r in range(OWN + 2):
        if r == 0:
            row = top[:, WIDTH:]
        elif r == OWN + 1:
            row = bot[:, 0:WIDTH]
        else:
            row = own[:, WIDTH * (r - 1) : WIDTH * r]
        wide = row.astype(F32)
        left = jnp.where(column == 0, 0.0, pltpu.roll(wide, 1, 1))
        right = jnp.where(column == WIDTH - 1, 0.0, pltpu.roll(wide, WIDTH - 1, 1))
        at = slice(16 * r, 16 * r + 16)
        taps[0, at] = left.astype(BF16)
        taps[1, at] = row
        taps[2, at] = right.astype(BF16)
    copies[1].wait()
    copies[2].wait()
    total = jnp.zeros((8, CH), F32)
    squares = jnp.zeros((8, CH), F32)
    for r in range(OWN):
        for half in range(2):
            cols = slice(512 * half, 512 * half + 512)
            patch = jnp.concatenate(
                [taps[b, 16 * (r + a) : 16 * (r + a) + 16, cols] for a in range(3) for b in range(3)],
                axis=0,
            )
            value = (dot_tn(patch, weight[...]) + bias[...]).reshape(64, 8, CH)
            total = total + jnp.sum(value, axis=0)
            squares = squares + jnp.sum(value * value, axis=0)
    channel = lax.broadcasted_iota(jnp.int32, (CH, 128), 0) // (CH // GROUPS)
    lane = lax.broadcasted_iota(jnp.int32, (CH, 128), 1)
    to_sum = jnp.where(channel == lane, 1.0, 0.0)
    to_squares = jnp.where(channel == lane - GROUPS, 1.0, 0.0)
    both = jnp.dot(
        total, to_sum, precision=lax.Precision.HIGHEST, preferred_element_type=F32
    ) + jnp.dot(squares, to_squares, precision=lax.Precision.HIGHEST, preferred_element_type=F32)
    out[...] = jnp.broadcast_to(jnp.sum(both, axis=0).reshape(1, 1, 128), (N_DEV, 1, 128))


def affine(stats, bias, gain, shift):
    sums = jnp.sum(stats[...], axis=0)
    sums = jnp.broadcast_to(sums, (8, 128)) / (TILE * TILE * N_DEV * (CH // GROUPS))
    channel = lax.broadcasted_iota(jnp.int32, (128, CH), 1) // (CH // GROUPS)
    lane = lax.broadcasted_iota(jnp.int32, (128, CH), 0)
    spread = functools.partial(
        jnp.dot, precision=lax.Precision.HIGHEST, preferred_element_type=F32
    )
    mean = spread(sums, jnp.where(channel == lane, 1.0, 0.0))[0:1]
    square = spread(sums, jnp.where(channel == lane - GROUPS, 1.0, 0.0))[0:1]
    scale = lax.rsqrt(square - mean * mean + EPSILON) * gain[...]
    return scale, (bias[...] - mean) * scale + shift[...]


def prepare_kernel(weight, points):
    def thirds(g):
        even = 0.5 * (g[0] + g[2])
        odd = 0.5 * g[1]
        return g[0], even + odd, even - odd, g[2]

    def transform(step, _):
        rows = pl.ds(pl.multiple_of(step * 16, 16), 16)
        for l in range(4):
            lanes = slice(128 * l, 128 * l + 128)
            columns = [
                thirds([weight[a, b, rows, lanes].astype(F32) for a in range(3)]) for b in range(3)
            ]
            for u in range(4):
                for v, value in enumerate(thirds([columns[b][u] for b in range(3)])):
                    points[4 * u + v, rows, lanes] = value.astype(BF16)
        return 0

    lax.fori_loop(0, weight.shape[2] // 16, transform, 0)


BLOCK = 8
N_BLOCK = TILE // 2 // BLOCK
M_ROWS = BLOCK * 32


def main_kernel(
    place,
    recv,
    stats,
    taps_hbm,
    bias_hbm,
    gain_hbm,
    shift_hbm,
    mid_bias_hbm,
    points_hbm,
    out_hbm,
    lat,
    act,
    affines,
    v0,
    v1,
    m0,
    m1,
    spread,
    out,
    taps,
    vectors,
    points,
    in_sems,
    sems,
):
    loads = start_copies(
        (taps_hbm, bias_hbm, gain_hbm, shift_hbm, mid_bias_hbm, points_hbm),
        (taps, *(vectors.at[i : i + 1] for i in range(4)), points),
        in_sems,
    )
    v_slots, m_slots = (v0, v1), (m0, m1)
    for s in range(N_COL):
        rows = recv[s].astype(F32)
        moved = [rows] + [pltpu.roll(rows, 128 - 16 * b, 1) for b in (1, 2)]
        for b in range(3):
            value = moved[b].astype(BF16)
            lat[b, 32 + 64 * s : 96 + 64 * s] = value[0:64]
            if s == 0:
                lat[b, 0:32] = value[64:96]
            if s == N_COL - 1:
                lat[b, 32 + 64 * N_COL :] = value[64:96]
    for load in loads[:-1]:
        load.wait()
    scale, offset = affine(stats, vectors[0:1], vectors[1:2], vectors[2:3])
    cell = lax.broadcasted_iota(jnp.int32, (16, CH), 0)
    hide_low = jnp.logical_and(cell == 0, place[1] == 0)
    hide_high = jnp.logical_and(cell == 15, place[1] == N_COL - 1)
    for i, value in enumerate((0.5 * scale, 0.5 * offset)):
        wide = jnp.broadcast_to(value, (16, CH))
        affines[i, 0] = jnp.where(hide_low, 0.0, wide)
        affines[i, 1] = wide
        affines[i, 2] = jnp.where(hide_high, 0.0, wide)

    def activate(pair):
        patches = []
        for j in range(2):
            at = pl.multiple_of((2 * pair + j) * 16, 16)
            patches.append(
                jnp.concatenate(
                    [lat[b, pl.ds(at + 16 * a, 16)] for a in range(3) for b in range(3)], axis=0
                )
            )
        value = dot_tn(jnp.concatenate(patches, axis=1), taps[...])
        for j in range(2):
            row = 2 * pair + j
            hidden = jnp.logical_or(
                jnp.logical_and(row == 0, place[0] == 0),
                jnp.logical_and(row == ACT - 1, place[0] == N_ROW - 1),
            )
            keep = jnp.where(hidden, 0.0, 1.0)
            for t in range(PLANES):
                kind = 0 if t == 0 else (2 if t == PLANES - 1 else 1)
                at = 128 * j + 16 * t
                half = value[at : at + 16] * (affines[0, kind] * keep) + affines[1, kind] * keep
                act[row, 16 * t : 16 * t + 16] = (half + half * jnp.tanh(half)).astype(BF16)

    def build(tile, slot):
        base = pl.multiple_of((tile % BLOCK) * 32, 32)
        for l in range(4):
            lanes = slice(128 * l, 128 * l + 128)
            rows = []
            for t in range(PLANES):
                d = [act[2 * tile + u, 16 * t : 16 * t + 16, lanes] for u in range(4)]
                rows.append((d[0] - d[2], d[1] + d[2], d[2] - d[1], d[1] - d[3]))
            for u in range(4):
                for q in range(2):
                    r = [rows[2 * q + v][u] for v in range(4)]
                    columns = (r[0] - r[2], r[1] + r[2], r[2] - r[1], r[1] - r[3])
                    for v in range(4):
                        slot[4 * u + v, pl.ds(base + 16 * q, 16), lanes] = columns[v]

    def multiply(point, v_slot, m_slot):
        m_slot[point] = dot_nt(v_slot[point], points[point])

    def finish(tile, slot):
        base = pl.multiple_of((tile % BLOCK) * 32, 32)
        for l in range(4):
            lanes = slice(128 * l, 128 * l + 128)
            bias = vectors[3:4, lanes]
            for q in range(2):
                sums = []
                for u in range(4):
                    m = [slot[4 * u + v, pl.ds(base + 16 * q, 16), lanes] for v in range(4)]
                    both, apart = m[1] + m[2], m[1] - m[2]
                    sums.append((m[0] + both, apart - m[3]))
                for f in range(2):
                    z = [sums[u][f] for u in range(4)]
                    both, apart = z[1] + z[2], z[1] - z[2]
                    spread[0, l, pl.ds(2 * q + f, 16, stride=4)] = z[0] + both + bias
                    spread[1, l, pl.ds(2 * q + f, 16, stride=4)] = apart - z[3] + bias
            for e in range(2):
                out[2 * tile + e, :, lanes] = spread[e, l].astype(BF16)

    activate(0)
    activate(1)

    def warm(c, _):
        build(c, v0)
        activate(c + 2)
        return 0

    lax.fori_loop(0, BLOCK, warm, 0)
    loads[-1].wait()
    last_pair = ACT // 2 - 1
    copies = []
    for n in range(N_BLOCK):
        this_v, next_v = v_slots[n % 2], v_slots[1 - n % 2]
        this_m, last_m = m_slots[n % 2], m_slots[1 - n % 2]

        def steady(c, _, n=n, this_v=this_v, next_v=next_v, this_m=this_m, last_m=last_m):
            g = n * BLOCK + c
            multiply(2 * c, this_v, this_m)
            if n > 0:
                finish(g - BLOCK, last_m)
            multiply(2 * c + 1, this_v, this_m)
            if n < N_BLOCK - 1:
                build(g + BLOCK, next_v)
                activate(jnp.minimum(g + BLOCK + 2, last_pair))
            return 0

        lax.fori_loop(0, BLOCK, steady, 0)
        if n > 0:
            copies.append(send(out, out_hbm, n - 1, sems))

    def drain(c, _):
        finish((N_BLOCK - 1) * BLOCK + c, m_slots[1 - N_BLOCK % 2])
        return 0

    lax.fori_loop(0, BLOCK, drain, 0)
    copies.append(send(out, out_hbm, N_BLOCK - 1, sems))
    for copy in copies:
        copy.wait()


def send(out, out_hbm, n, sems):
    rows = slice(2 * BLOCK * n, 2 * BLOCK * (n + 1))
    copy = pltpu.make_async_copy(out.at[rows], out_hbm.at[rows], sems.at[n])
    copy.start()
    return copy


def step(latent, in_weight, in_bias, norm_gain, norm_shift, mid_weight, mid_bias):
    both = ("row", "col")
    up = [(i, i + 1) for i in range(N_DEV - 1)]
    down = [(i + 1, i) for i in range(N_DEV - 1)]
    top = lax.ppermute(latent[:, 2 * WIDTH :], both, up)
    bot = lax.ppermute(latent[:, : 2 * WIDTH], both, down)
    taps = in_weight.reshape(9 * C_LAT, CH)
    bias = in_bias.reshape(1, CH)
    place = jnp.stack([lax.axis_index("row"), lax.axis_index("col")]).astype(jnp.int32)
    chunks = pl.pallas_call(
        pack_kernel,
        out_shape=jax.ShapeDtypeStruct((N_COL, 96, 128), BF16),
        in_specs=[SMEM, HBM, VMEM, VMEM],
        out_specs=VMEM,
        scratch_shapes=[
            pltpu.VMEM((96, WIDTH), BF16),
            pltpu.VMEM((C_LAT, OWN * WIDTH), BF16),
            pltpu.SemaphoreType.DMA((1,)),
        ],
        compiler_params=pltpu.CompilerParams(vmem_limit_bytes=8 * MIB),
        name="pack",
    )(place, hbm(latent), top, bot)
    recv = lax.all_to_all(chunks, "col", split_axis=0, concat_axis=0, tiled=True)
    partial = pl.pallas_call(
        stats_kernel,
        out_shape=jax.ShapeDtypeStruct((N_DEV, 1, 128), F32),
        in_specs=[HBM, VMEM, VMEM, HBM, HBM],
        out_specs=VMEM,
        scratch_shapes=[
            pltpu.VMEM((3, 96, WIDTH), BF16),
            pltpu.VMEM((C_LAT, OWN * WIDTH), BF16),
            pltpu.VMEM((9 * C_LAT, CH), BF16),
            pltpu.VMEM((1, CH), F32),
            pltpu.SemaphoreType.DMA((3,)),
        ],
        compiler_params=pltpu.CompilerParams(vmem_limit_bytes=12 * MIB),
        name="stats",
    )(hbm(latent), top, bot, hbm(taps), hbm(bias))
    stats = lax.all_to_all(partial, both, split_axis=0, concat_axis=0, tiled=True)
    points = pl.pallas_call(
        prepare_kernel,
        out_shape=jax.ShapeDtypeStruct((16, CH, CH), BF16),
        grid=(8,),
        in_specs=[pl.BlockSpec((3, 3, CH // 8, CH), lambda i: (0, 0, i, 0))],
        out_specs=pl.BlockSpec((16, CH // 8, CH), lambda i: (0, i, 0)),
        compiler_params=pltpu.CompilerParams(vmem_limit_bytes=60 * MIB),
        name="prepare",
    )(hbm(jnp.transpose(mid_weight, (1, 2, 0, 3))))
    return pl.pallas_call(
        main_kernel,
        out_shape=jax.ShapeDtypeStruct((TILE, TILE, CH), BF16),
        in_specs=[SMEM, VMEM, VMEM] + [HBM] * 6,
        out_specs=HBM,
        scratch_shapes=[
            pltpu.VMEM((3, LAT * 16, 128), BF16),
            pltpu.VMEM((ACT, PLANES * 16, CH), BF16),
            pltpu.VMEM((2, 3, 16, CH), F32),
            pltpu.VMEM((16, M_ROWS, CH), BF16),
            pltpu.VMEM((16, M_ROWS, CH), BF16),
            pltpu.VMEM((16, M_ROWS, CH), F32),
            pltpu.VMEM((16, M_ROWS, CH), F32),
            pltpu.VMEM((2, 4, TILE, 128), F32),
            pltpu.VMEM((TILE, TILE, CH), BF16),
            pltpu.VMEM((9 * C_LAT, CH), BF16),
            pltpu.VMEM((4, CH), F32),
            pltpu.VMEM((16, CH, CH), BF16),
            pltpu.SemaphoreType.DMA((6,)),
            pltpu.SemaphoreType.DMA((N_BLOCK,)),
        ],
        compiler_params=pltpu.CompilerParams(vmem_limit_bytes=52 * MIB),
        name="main",
    )(
        place,
        recv,
        stats,
        hbm(taps),
        hbm(bias),
        hbm(norm_gain.reshape(1, CH)),
        hbm(norm_shift.reshape(1, CH)),
        hbm(mid_bias.reshape(1, CH)),
        hbm(points),
    )


def solution(mesh):
    in_specs = (P(None, ("row", "col")), P(), P(), P(), P(), P(), P())
    return jax.shard_map(
        step, mesh=mesh, in_specs=in_specs, out_specs=P("row", "col", None), check_vma=False
    )
```

time: 87 us -> 77.9 us (0.90)
  waiting for transfers between devices: 17.1 us -> 8.21 us
  local copies, waits for them, and re-layouts: 9.07 us -> 0.88 us
  Pallas kernels: 34.7 us -> 42.4 us
    all_to_all x2, waiting for transfers between devices: 17.1 us -> 6.91 us  [the longest x1 6.91 us: step(): lax.all_to_all(partial, both, split_axis=0, concat_axis=0, tiled=True)]
    pallas_call x3 -> x4, Pallas kernels: 34.7 us -> 42.4 us  [the longest x1 27.8 us: step(): pl.pallas_call(main_kernel, out_shape=jax.ShapeDtypeStruct((TILE, TILE, C...]
    unnamed x16 -> x0, local copies, waits for them, and re-layouts: 6.61 us -> none
    transpose x1 -> x0, local copies, waits for them, and re-layouts: 1.59 us -> none  [body(): taps = jnp.transpose(in_weight, (1, 0, 2, 3)).reshape(9 * C_LAT, CH)]
    ppermute x2, waiting for transfers between devices: 0.01 us -> 1.3 us  [the longest x1 1.29 us: step(): top = lax.ppermute(latent[:, 2 * WIDTH:], both, up)]
  transfers between devices with their start and end apart: 4 -> 4, of which waited for: 2 -> 2; matrix products, arithmetic and copies ran while one was open for 2% -> 0% of each run, Pallas kernels for 3% -> 14%
where the time goes in v1:
time: 77.9 us; the launch traced here: 77.4 us
  Pallas kernels  42.4 us (54%)
  starting transfers between devices  25.8 us (33%)
  waiting for transfers between devices  8.21 us (11%)
  local copies, waits for them, and re-layouts  0.88 us (1%)
    pallas_call x1, Pallas kernels, step(): pl.pallas_call(main_kernel, out_shape=jax.ShapeDtypeStruct((TILE, TILE, C...  27.8 us
    all_to_all x1, starting transfers between devices, step(): lax.all_to_all(partial, both, split_axis=0, concat_axis=0, tiled=True)  15.3 us
    pallas_call x1, Pallas kernels, step(): pl.pallas_call(prepare_kernel, out_shape=jax.ShapeDtypeStruct((16, CH, CH...  8.35 us
    all_to_all x1, waiting for transfers between devices, step(): lax.all_to_all(partial, both, split_axis=0, concat_axis=0, tiled=True)  6.91 us
    all_to_all x1, starting transfers between devices, step(): lax.all_to_all(chunks, 'col', split_axis=0, concat_axis=0, tiled=True)  4.11 us
    pallas_call x1, Pallas kernels, step(): pl.pallas_call(stats_kernel, out_shape=jax.ShapeDtypeStruct((N_DEV, 1, 12...  3.62 us
    ppermute x1, starting transfers between devices, step(): bot = lax.ppermute(latent[:, :2 * WIDTH], both, down)  3.29 us
    ppermute x1, starting transfers between devices, step(): top = lax.ppermute(latent[:, 2 * WIDTH:], both, up)  3.13 us
  transfers between devices with their start and end apart: 4, of which 2 were waited for; matrix products, arithmetic and copies ran while one was open for 0% of the time, Pallas kernels for 14%

profile of v1, /device:TPU:1, one launch (start us, length us, event | category | flops | bytes accessed | tf_op | source)
XLA Modules:
  0.0 77.4 jit_solution(1699724796028427215)
XLA Ops:
  0.0 0.9 %fusion = (bf16[16,2048]{1,0:T(8,128)(2,1)S(1)}, bf16[16,2048]{1,0:T(8,128)(2,1)S(1)}) fusion(bf16[16,4096]{1,0:T(8,128)(2,1)} %own_hbm.3), kind=kLoop, calls=%fused_computation.1 | loop fusion | bytes 262144 | tf_op jit(solution)/shard_map/slice | solution.py:333
  0.9 3.3 %collective-permute-start.1 = (bf16[16,2048]{1,0:T(8,128)(2,1)S(1)}, bf16[16,2048]{1,0:T(8,128)(2,1)S(1)}, u32[]{:S(2)}, u32[]{:S(2)}) collective-permute-start(bf16[16,2048]{1,0:T(8,128)(2,1)S(1)} %get-tuple-element.5), channel_id=1, source_target_pairs={{1,0},{2,1},{3,2},{4,3},{5,4},{6,5},{7,6},{8,7},{9,8},{10,9},{11,1... | collective-permute-start | bytes 196616 | tf_op jit(solution)/shard_map/ppermute | solution.py:333
  4.2 3.1 %collective-permute-start = (bf16[16,2048]{1,0:T(8,128)(2,1)S(1)}, bf16[16,2048]{1,0:T(8,128)(2,1)S(1)}, u32[]{:S(2)}, u32[]{:S(2)}) collective-permute-start(bf16[16,2048]{1,0:T(8,128)(2,1)S(1)} %get-tuple-element.6), channel_id=1, source_target_pairs={{0,1},{1,2},{2,3},{3,4},{4,5},{5,6},{6,7},{7,8},{8,9},{9,10},{10,1... | collective-permute-start | bytes 196616 | tf_op jit(solution)/shard_map/ppermute | solution.py:332
  7.3 0.0 collective-permute-done.1.bot
  7.3 1.3 %collective-permute-done.top = bf16[16,2048]{1,0:T(8,128)(2,1)S(1)} collective-permute-done((bf16[16,2048]{1,0:T(8,128)(2,1)S(1)}, bf16[16,2048]{1,0:T(8,128)(2,1)S(1)}, u32[]{:S(2)}, u32[]{:S(2)}) %collective-permute-start) | collective-permute-done | bytes 65568 | tf_op jit(solution)/shard_map/ppermute | solution.py:332
  8.6 3.6 %stats.1 = f32[128,1,128]{2,1,0:T(1,128)} custom-call(bf16[16,4096]{1,0:T(8,128)(2,1)} %own_hbm.3, bf16[16,2048]{1,0:T(8,128)(2,1)S(1)} %collective-permute-done.top, bf16[16,2048]{1,0:T(8,128)(2,1)S(1)} %collective-permute-done.1.bot, bf16[144,512]{1,0:T(8,128)(2,1)} %bitcast.9, f32[1,512]{1,0:T(1,128)} %bitcast.11), custom_call_target="tpu_custom_call" | custom-call | tf_op jit(solution)/shard_map/stats/pallas_call | solution.py:351
  12.3 15.3 %all-to-all-start.1 = ((f32[128,1,128]{2,1,0:T(1,128)}), f32[128,1,128]{2,1,0:T(1,128)S(1)}, u32[]{:S(2)}, u32[]{:S(2)}) async-start(f32[128,1,128]{2,1,0:T(1,128)} %stats.1), calls=%async_computation.1 | async-start | bytes 131072 | tf_op jit(solution)/shard_map/all_to_all | solution.py:366
  27.5 0.1 pad_add_fusion.place
  27.6 2.6 %pack.1 = bf16[16,96,128]{2,1,0:T(8,128)(2,1)} custom-call(s32[2]{0:T(128)S(1)} %pad_add_fusion.place, bf16[16,4096]{1,0:T(8,128)(2,1)} %own_hbm.3, bf16[16,2048]{1,0:T(8,128)(2,1)S(1)} %collective-permute-done.top, bf16[16,2048]{1,0:T(8,128)(2,1)S(1)} %collective-permute-done.1.bot), custom_call_target="tpu_custom_call" | custom-call | tf_op jit(solution)/shard_map/pack/pallas_call | solution.py:337
  30.2 6.9 %all-to-all-done.1.stats = f32[128,1,128]{2,1,0:T(1,128)S(1)} async-done(((f32[128,1,128]{2,1,0:T(1,128)}), f32[128,1,128]{2,1,0:T(1,128)S(1)}, u32[]{:S(2)}, u32[]{:S(2)}) %all-to-all-start.1) | async-done | bytes 65568 | tf_op jit(solution)/shard_map/all_to_all | solution.py:366
  37.1 4.1 %all-to-all-start = ((bf16[16,96,128]{2,1,0:T(8,128)(2,1)}), bf16[16,96,128]{2,1,0:T(8,128)(2,1)S(1)}, u32[]{:S(2)}, u32[]{:S(2)}) async-start(bf16[16,96,128]{2,1,0:T(8,128)(2,1)} %pack.1), calls=%async_computation | async-start | bytes 786432 | tf_op jit(solution)/shard_map/all_to_all | solution.py:350
  41.2 8.4 %prepare.1.points_hbm = bf16[16,512,512]{2,1,0:T(8,128)(2,1)} custom-call(bf16[3,3,512,512]{3,2,1,0:T(8,128)(2,1)} %bitcast.8), custom_call_target="tpu_custom_call" | custom-call | tf_op jit(solution)/shard_map/prepare/pallas_call | solution.py:367
  49.6 0.0 all-to-all-done.recv
  49.6 27.8 %main.1 = bf16[64,64,512]{2,1,0:T(8,128)(2,1)} custom-call(s32[2]{0:T(128)S(1)} %pad_add_fusion.place, bf16[16,96,128]{2,1,0:T(8,128)(2,1)S(1)} %all-to-all-done.recv, f32[128,1,128]{2,1,0:T(1,128)S(1)} %all-to-all-done.1.stats, bf16[144,512]{1,0:T(8,128)(2,1)} %bitcast.10, f32[1,512]{1,0:T(1,128)} %bitcast.12, f32[1,512]{1,0:T(1,128)} %bitcast.13, ...), custom_call_target="tpu_custom_call" | custom-call | tf_op jit(solution)/shard_map/main/pallas_call | solution.py:376
Async XLA Ops:
  0.9 6.4 %collective-permute-start.1 = (bf16[16,2048]{1,0:T(8,128)(2,1)S(1)}, bf16[16,2048]{1,0:T(8,128)(2,1)S(1)}, u32[]{:S(2)}, u32[]{:S(2)}) collective-permute-start(bf16[16,2048]{1,0:T(8,128)(2,1)S(1)} %get-tuple-element.5), channel_id=1, source_target_pairs={{1,0},{2,1},{3,2},{4,3},{5,4},{6,5},{7,6},{8,7},{9,8},{10,9},{11,1... | collective-permute-start | bytes 196616 | tf_op jit(solution)/shard_map/ppermute | solution.py:333
  4.2 4.4 %collective-permute-start = (bf16[16,2048]{1,0:T(8,128)(2,1)S(1)}, bf16[16,2048]{1,0:T(8,128)(2,1)S(1)}, u32[]{:S(2)}, u32[]{:S(2)}) collective-permute-start(bf16[16,2048]{1,0:T(8,128)(2,1)S(1)} %get-tuple-element.6), channel_id=1, source_target_pairs={{0,1},{1,2},{2,3},{3,4},{4,5},{5,6},{6,7},{7,8},{8,9},{9,10},{10,1... | collective-permute-start | bytes 196616 | tf_op jit(solution)/shard_map/ppermute | solution.py:332
  12.3 24.9 %all-to-all-start.1 = ((f32[128,1,128]{2,1,0:T(1,128)}), f32[128,1,128]{2,1,0:T(1,128)S(1)}, u32[]{:S(2)}, u32[]{:S(2)}) async-start(f32[128,1,128]{2,1,0:T(1,128)} %stats.1), calls=%async_computation.1 | async-start | bytes 131072 | tf_op jit(solution)/shard_map/all_to_all | solution.py:366
  37.1 12.5 %all-to-all-start = ((bf16[16,96,128]{2,1,0:T(8,128)(2,1)}), bf16[16,96,128]{2,1,0:T(8,128)(2,1)S(1)}, u32[]{:S(2)}, u32[]{:S(2)}) async-start(bf16[16,96,128]{2,1,0:T(8,128)(2,1)} %pack.1), calls=%async_computation | async-start | bytes 786432 | tf_op jit(solution)/shard_map/all_to_all | solution.py:350

commit v2 on v1

v2 whole, which is shorter than its diff:
```python
import functools

import jax
import jax.numpy as jnp
from jax import lax
from jax.experimental import pallas as pl
from jax.experimental.pallas import tpu as pltpu
from jax.sharding import PartitionSpec as P

C_LAT = 16
CH = 512
GROUPS = 32
TILE = 64
WIDTH = 1024
N_ROW = 8
N_COL = 16
N_DEV = N_ROW * N_COL
OWN = 4
ACT = TILE + 2
LAT = TILE + 4
PLANES = 6
EPSILON = 1e-06
BF16 = jnp.bfloat16
F32 = jnp.float32
VMEM = pl.BlockSpec(memory_space=pltpu.VMEM)
SMEM = pl.BlockSpec(memory_space=pltpu.SMEM)
HBM = pl.BlockSpec(memory_space=pltpu.HBM)
MIB = 1 << 20


def dot_tn(lhs, rhs):
    return lax.dot_general(lhs, rhs, (((0,), (0,)), ((), ())), preferred_element_type=F32)


def dot_nt(lhs, rhs):
    return lax.dot_general(lhs, rhs, (((1,), (1,)), ((), ())), preferred_element_type=F32)


def hbm(array):
    return pltpu.with_memory_space_constraint(array, pltpu.HBM)


def start_copies(sources, targets, sems):
    copies = [
        pltpu.make_async_copy(source, target, sems.at[i])
        for i, (source, target) in enumerate(zip(sources, targets))
    ]
    for copy in copies:
        copy.start()
    return copies


def pack_kernel(own_hbm, out, rows, own, sems):
    copies = start_copies((own_hbm,), (own,), sems)
    k = lax.broadcasted_iota(jnp.int32, (384, 256), 0)
    n = lax.broadcasted_iota(jnp.int32, (384, 256), 1)
    lane = n % 128
    column = 64 * (n // 128) + 4 * (lane % 16) + lane // 16 + 126
    pick = jnp.where(k == column, 1.0, 0.0).astype(BF16)
    zero = jnp.zeros((64, 128), BF16)
    copies[0].wait()
    for r in range(OWN):
        rows[16 * r : 16 * r + 16] = own[:, WIDTH * r : WIDTH * (r + 1)]
    for t in range(8):
        parts = [
            rows[:, 128 * u : 128 * (u + 1)] if 0 <= u < 8 else zero for u in (t - 1, t, t + 1)
        ]
        moved = jnp.dot(jnp.concatenate(parts, axis=1), pick, preferred_element_type=F32)
        out[2 * t] = moved[:, :128].astype(BF16)
        out[2 * t + 1] = moved[:, 128:].astype(BF16)


def add_cells(value, total, squares):
    value = value.reshape(value.shape[0] // 8, 8, CH)
    return total + jnp.sum(value, axis=0), squares + jnp.sum(value * value, axis=0)


def inner_kernel(recv, weight_hbm, bias_hbm, sums, pairs, weight, bias, sems):
    copies = start_copies((weight_hbm, bias_hbm), (weight, bias), sems)
    rows = recv[...].astype(F32)
    low = lax.broadcasted_iota(jnp.int32, (16 * (TILE - 1), 128), 1) < 64
    for b in range(3):
        even = pltpu.roll(rows, 112 - 16 * b, 1)
        odd = pltpu.roll(rows, (176 - 16 * b) % 128, 1)
        pairs[b] = jnp.where(low, even[:-16], odd[16:]).astype(BF16)
    for copy in copies:
        copy.wait()
    taps = weight[...]
    shift = bias[...]

    def accumulate(first, count, carry):
        patches = [
            jnp.concatenate(
                [
                    pairs[b, pl.ds(pl.multiple_of((2 * (first + j) + a) * 16, 16), 16)]
                    for a in range(3)
                    for b in range(3)
                ],
                axis=0,
            )
            for j in range(count)
        ]
        return add_cells(dot_tn(jnp.concatenate(patches, axis=1), taps) + shift, *carry)

    zero = jnp.zeros((8, CH), F32)
    carry = lax.fori_loop(0, 7, lambda i, c: accumulate(4 * i, 4, c), (zero, zero))
    sums[0], sums[1] = accumulate(28, 3, carry)


def rim_rows(place, rim):
    top = rim[jnp.maximum(place[0] - 1, 0)].astype(F32)
    bot = rim[jnp.minimum(place[0] + 1, N_ROW - 1)].astype(F32)
    top = jnp.where(place[0] == 0, 0.0, top)
    return top, jnp.where(place[0] == N_ROW - 1, 0.0, bot)


def outer_kernel(place, recv, rim, sums, weight_hbm, bias_hbm, out, weight, bias, sems):
    copies = start_copies((weight_hbm, bias_hbm), (weight, bias), sems)
    channel = lax.broadcasted_iota(jnp.int32, (CH, 128), 0) // (CH // GROUPS)
    lane = lax.broadcasted_iota(jnp.int32, (CH, 128), 1)
    to_sum = jnp.where(channel == lane, 1.0, 0.0)
    to_squares = jnp.where(channel == lane - GROUPS, 1.0, 0.0)
    top, bot = rim_rows(place, rim)
    first = jnp.concatenate([top[16:], recv[0:32].astype(F32)], axis=0)
    last = jnp.concatenate([recv[16 * TILE - 32 :].astype(F32), bot[:16]], axis=0)
    low = lax.broadcasted_iota(jnp.int32, (48, 128), 1) < 64
    shifted = [
        jnp.where(
            low, pltpu.roll(first, 112 - 16 * b, 1), pltpu.roll(last, (176 - 16 * b) % 128, 1)
        ).astype(BF16)
        for b in range(3)
    ]
    patch = jnp.concatenate(
        [shifted[b][16 * a : 16 * a + 16] for a in range(3) for b in range(3)], axis=0
    )
    for copy in copies:
        copy.wait()
    total, squares = add_cells(dot_tn(patch, weight[...]) + bias[...], sums[0], sums[1])
    exact = functools.partial(
        jnp.dot, precision=lax.Precision.HIGHEST, preferred_element_type=F32
    )
    both = exact(total, to_sum) + exact(squares, to_squares)
    out[...] = jnp.broadcast_to(jnp.sum(both, axis=0).reshape(1, 1, 128), (N_DEV, 1, 128))


def affine(stats, bias, gain, shift):
    sums = jnp.sum(stats[...], axis=0)
    sums = jnp.broadcast_to(sums, (8, 128)) / (TILE * TILE * N_DEV * (CH // GROUPS))
    channel = lax.broadcasted_iota(jnp.int32, (128, CH), 1) // (CH // GROUPS)
    lane = lax.broadcasted_iota(jnp.int32, (128, CH), 0)
    spread = functools.partial(
        jnp.dot, precision=lax.Precision.HIGHEST, preferred_element_type=F32
    )
    mean = spread(sums, jnp.where(channel == lane, 1.0, 0.0))[0:1]
    square = spread(sums, jnp.where(channel == lane - GROUPS, 1.0, 0.0))[0:1]
    scale = lax.rsqrt(square - mean * mean + EPSILON) * gain[...]
    return scale, (bias[...] - mean) * scale + shift[...]


def prepare_kernel(weight, points):
    def thirds(g):
        even = 0.5 * (g[0] + g[2])
        odd = 0.5 * g[1]
        return g[0], even + odd, even - odd, g[2]

    def transform(step, _):
        rows = pl.ds(pl.multiple_of(step * 16, 16), 16)
        for l in range(4):
            lanes = slice(128 * l, 128 * l + 128)
            columns = [
                thirds([weight[a, b, rows, lanes].astype(F32) for a in range(3)]) for b in range(3)
            ]
            for u in range(4):
                for v, value in enumerate(thirds([columns[b][u] for b in range(3)])):
                    points[4 * u + v, rows, lanes] = value.astype(BF16)
        return 0

    lax.fori_loop(0, weight.shape[2] // 16, transform, 0)


BLOCK = 8
TILES = 4
N_BLOCK = TILE // 2 // BLOCK
M_ROWS = BLOCK * 32


def main_kernel(
    place,
    recv,
    rim,
    stats,
    taps_hbm,
    bias_hbm,
    gain_hbm,
    shift_hbm,
    mid_bias_hbm,
    low_hbm,
    high_hbm,
    out_hbm,
    lat,
    act,
    affines,
    raw,
    v0,
    v1,
    m0,
    m1,
    spread,
    out,
    taps,
    vectors,
    points,
    in_sems,
    sems,
):
    loads = start_copies(
        (taps_hbm, bias_hbm, gain_hbm, shift_hbm, mid_bias_hbm, low_hbm, high_hbm),
        (
            taps,
            *(vectors.at[i : i + 1] for i in range(4)),
            points.at[:, : CH // 2],
            points.at[:, CH // 2 :],
        ),
        in_sems,
    )
    v_slots, m_slots = (v0, v1), (m0, m1)

    def place_rows(at, rows):
        for b in range(3):
            value = rows if b == 0 else pltpu.roll(rows, 128 - 16 * b, 1)
            lat[b, at : at + rows.shape[0]] = value.astype(BF16)

    top, bot = rim_rows(place, rim)
    place_rows(0, top)
    for r in range(0, 16 * TILE, 64):
        place_rows(32 + r, recv[r : r + 64].astype(F32))
    place_rows(32 + 16 * TILE, bot)
    for load in loads[:-2]:
        load.wait()
    scale, offset = affine(stats, vectors[0:1], vectors[1:2], vectors[2:3])
    cell = lax.broadcasted_iota(jnp.int32, (16, CH), 0)
    hide_low = jnp.logical_and(cell == 0, place[1] == 0)
    hide_high = jnp.logical_and(cell == 15, place[1] == N_COL - 1)
    for i, value in enumerate((0.5 * scale, 0.5 * offset)):
        wide = jnp.broadcast_to(value, (16, CH))
        affines[i, 0] = jnp.where(hide_low, 0.0, wide)
        affines[i, 1] = wide
        affines[i, 2] = jnp.where(hide_high, 0.0, wide)
        affines[i, 3] = jnp.zeros((16, CH), F32)

    def contract(pair):
        patches = []
        for j in range(2):
            at = pl.multiple_of((2 * pair + j) * 16, 16)
            patches.append(
                jnp.concatenate(
                    [lat[b, pl.ds(at + 16 * a, 16)] for a in range(3) for b in range(3)], axis=0
                )
            )
        raw[...] = dot_tn(jnp.concatenate(patches, axis=1), taps[...])

    def activate(pair, pieces=range(4)):
        for j in range(2):
            row = 2 * pair + j
            hidden = jnp.logical_or(
                jnp.logical_and(row == 0, place[0] == 0),
                jnp.logical_and(row == ACT - 1, place[0] == N_ROW - 1),
            )
            for l in pieces:
                lanes = slice(128 * l, 128 * l + 128)
                for t in range(PLANES):
                    kind = jnp.where(hidden, 3, 0 if t == 0 else (2 if t == PLANES - 1 else 1))
                    at = 128 * j + 16 * t
                    half = raw[at : at + 16, lanes] * affines[0, kind, :, lanes]
                    half = half + affines[1, kind, :, lanes]
                    act[row, l, 16 * t : 16 * t + 16] = (half + half * jnp.tanh(half)).astype(BF16)

    def build(tile, slot, pieces=range(4)):
        base = pl.multiple_of((tile % BLOCK) * 32, 32)
        for l in pieces:
            rows = []
            for q in range(2):
                for t in range(len(rows), 4 + 2 * q):
                    d = [act[2 * tile + u, l, 16 * t : 16 * t + 16] for u in range(4)]
                    rows.append((d[0] - d[2], d[1] + d[2], d[2] - d[1], d[1] - d[3]))
                for u in range(4):
                    r = [rows[2 * q + v][u] for v in range(4)]
                    columns = (r[0] - r[2], r[1] + r[2], r[2] - r[1], r[1] - r[3])
                    for v in range(4):
                        slot[4 * u + v, l, pl.ds(base + 16 * q, 16)] = columns[v]

    def multiply(point, v_slot, m_slot, half):
        cells = jnp.concatenate([v_slot[point, l] for l in range(4)], axis=1)
        value = dot_nt(cells, points[point, 256 * half : 256 * half + 256])
        for i in range(2):
            m_slot[point, 2 * half + i] = value[:, 128 * i : 128 * i + 128]

    def finish(tile, slot, pieces=range(4)):
        base = pl.multiple_of((tile % BLOCK) * 32, 32)
        for l in pieces:
            bias = vectors[3:4, 128 * l : 128 * l + 128]
            for q in range(2):
                for h in range(2):
                    sums = []
                    for u in range(4):
                        m = [slot[4 * u + v, l, pl.ds(base + 16 * q + 8 * h, 8)] for v in range(4)]
                        both, apart = m[1] + m[2], m[1] - m[2]
                        sums.append((m[0] + both, apart - m[3]))
                    for f in range(2):
                        z = [sums[u][f] for u in range(4)]
                        both, apart = z[1] + z[2], z[1] - z[2]
                        at = pl.ds(32 * h + 2 * q + f, 8, stride=4)
                        spread[0, l, at] = z[0] + both + bias
                        spread[1, l, at] = apart - z[3] + bias
            for e in range(2):
                out[2 * tile + e, l] = spread[e, l].astype(BF16)

    for pair in range(2):
        contract(pair)
        activate(pair)

    def warm(c, _):
        contract(c + 2)
        build(c, v0)
        activate(c + 2)
        return 0

    lax.fori_loop(0, BLOCK, warm, 0)
    loads[-2].wait()
    loads[-1].wait()
    last_pair = ACT // 2 - 1
    copies = []
    for n in range(N_BLOCK):
        this_v, next_v = v_slots[n % 2], v_slots[1 - n % 2]
        this_m, last_m = m_slots[n % 2], m_slots[1 - n % 2]

        def steady(c, _, n=n, this_v=this_v, next_v=next_v, this_m=this_m, last_m=last_m):
            first = n * BLOCK + c * TILES
            ahead = n < N_BLOCK - 1
            for k in range(TILES):
                g = first + k
                pair = jnp.minimum(g + BLOCK + 2, last_pair)
                if ahead:
                    contract(pair)
                for i in range(4):
                    multiply(2 * (c * TILES + k) + i // 2, this_v, this_m, i % 2)
                    if n > 0:
                        finish(g - BLOCK, last_m, (i,))
                    if ahead:
                        build(g + BLOCK, next_v, (i,))
                        activate(pair, (i,))
            return 0

        lax.fori_loop(0, BLOCK // TILES, steady, 0)
        if n > 0:
            copies.extend(send(out, out_hbm, n - 1, sems))

    def drain(c, _):
        finish((N_BLOCK - 1) * BLOCK + c, m_slots[1 - N_BLOCK % 2])
        return 0

    lax.fori_loop(0, BLOCK, drain, 0)
    copies.extend(send(out, out_hbm, N_BLOCK - 1, sems))
    for copy in copies:
        copy.wait()


def send(out, out_hbm, n, sems):
    rows = slice(2 * BLOCK * n, 2 * BLOCK * (n + 1))
    copies = [
        pltpu.make_async_copy(
            out.at[rows, l], out_hbm.at[rows, :, 128 * l : 128 * l + 128], sems.at[n, l]
        )
        for l in range(4)
    ]
    for copy in copies:
        copy.start()
    return copies


def step(latent, in_weight, in_bias, norm_gain, norm_shift, mid_weight, mid_bias):
    both = ("row", "col")
    taps = in_weight.reshape(9 * C_LAT, CH)
    bias = in_bias.reshape(1, CH)
    place = jnp.stack([lax.axis_index("row"), lax.axis_index("col")]).astype(jnp.int32)
    weights = [pltpu.VMEM((9 * C_LAT, CH), BF16), pltpu.VMEM((1, CH), F32)]
    small = pltpu.CompilerParams(vmem_limit_bytes=12 * MIB)
    chunks = pl.pallas_call(
        pack_kernel,
        out_shape=jax.ShapeDtypeStruct((N_COL, 64, 128), BF16),
        in_specs=[HBM],
        out_specs=VMEM,
        scratch_shapes=[
            pltpu.VMEM((64, WIDTH), BF16),
            pltpu.VMEM((C_LAT, OWN * WIDTH), BF16),
            pltpu.SemaphoreType.DMA((1,)),
        ],
        compiler_params=small,
        name="pack",
    )(hbm(latent))
    recv = lax.all_to_all(chunks, "col", split_axis=0, concat_axis=0, tiled=True)
    recv = recv.reshape(16 * TILE, 128)
    above = lax.broadcasted_iota(jnp.int32, (N_ROW, 32, 128), 0) > place[0]
    edges = jnp.where(above, recv[None, -32:], recv[None, :32])
    rim = lax.all_to_all(edges, "row", split_axis=0, concat_axis=0, tiled=True)
    sums = pl.pallas_call(
        inner_kernel,
        out_shape=jax.ShapeDtypeStruct((2, 8, CH), F32),
        in_specs=[VMEM, HBM, HBM],
        out_specs=VMEM,
        scratch_shapes=[pltpu.VMEM((3, 16 * (TILE - 1), 128), BF16)]
        + weights
        + [pltpu.SemaphoreType.DMA((2,))],
        compiler_params=small,
        name="inner",
    )(recv, hbm(taps), hbm(bias))
    partial = pl.pallas_call(
        outer_kernel,
        out_shape=jax.ShapeDtypeStruct((N_DEV, 1, 128), F32),
        in_specs=[SMEM, VMEM, VMEM, VMEM, HBM, HBM],
        out_specs=VMEM,
        scratch_shapes=weights + [pltpu.SemaphoreType.DMA((2,))],
        compiler_params=small,
        name="outer",
    )(place, recv, rim, sums, hbm(taps), hbm(bias))
    stats = lax.all_to_all(partial, both, split_axis=0, concat_axis=0, tiled=True)
    weight = hbm(jnp.transpose(mid_weight, (1, 2, 0, 3)))
    points = []
    for part in range(2):
        points.append(
            pl.pallas_call(
                prepare_kernel,
                out_shape=jax.ShapeDtypeStruct((16, CH // 2, CH), BF16),
                grid=(4,),
                in_specs=[
                    pl.BlockSpec((3, 3, CH // 8, CH), lambda i, part=part: (0, 0, i + 4 * part, 0))
                ],
                out_specs=pl.BlockSpec((16, CH // 8, CH), lambda i: (0, i, 0)),
                compiler_params=pltpu.CompilerParams(vmem_limit_bytes=60 * MIB),
            )(weight)
        )
    return pl.pallas_call(
        main_kernel,
        out_shape=jax.ShapeDtypeStruct((TILE, TILE, CH), BF16),
        in_specs=[SMEM, VMEM, VMEM, VMEM] + [HBM] * 7,
        out_specs=HBM,
        scratch_shapes=[
            pltpu.VMEM((3, LAT * 16, 128), BF16),
            pltpu.VMEM((ACT, 4, PLANES * 16, 128), BF16),
            pltpu.VMEM((2, 4, 16, CH), F32),
            pltpu.VMEM((256, CH), F32),
            pltpu.VMEM((16, 4, M_ROWS, 128), BF16),
            pltpu.VMEM((16, 4, M_ROWS, 128), BF16),
            pltpu.VMEM((16, 4, M_ROWS, 128), F32),
            pltpu.VMEM((16, 4, M_ROWS, 128), F32),
            pltpu.VMEM((2, 4, TILE, 128), F32),
            pltpu.VMEM((TILE, 4, TILE, 128), BF16),
            pltpu.VMEM((9 * C_LAT, CH), BF16),
            pltpu.VMEM((4, CH), F32),
            pltpu.VMEM((16, CH, CH), BF16),
            pltpu.SemaphoreType.DMA((7,)),
            pltpu.SemaphoreType.DMA((N_BLOCK, 4)),
        ],
        compiler_params=pltpu.CompilerParams(vmem_limit_bytes=52 * MIB),
        name="main",
    )(
        place,
        recv,
        rim,
        stats,
        hbm(taps),
        hbm(bias),
        hbm(norm_gain.reshape(1, CH)),
        hbm(norm_shift.reshape(1, CH)),
        hbm(mid_bias.reshape(1, CH)),
        hbm(points[0]),
        hbm(points[1]),
    )


def solution(mesh):
    in_specs = (P(None, ("row", "col")), P(), P(), P(), P(), P(), P())
    return jax.shard_map(
        step, mesh=mesh, in_specs=in_specs, out_specs=P("row", "col", None), check_vma=False
    )
```

time: 77.9 us -> 72.1 us (0.926)
  starting transfers between devices: 25.8 us -> 19.9 us
  waiting for transfers between devices: 8.21 us -> 10.3 us
  Pallas kernels: 42.4 us -> 40.6 us
  local copies, waits for them, and re-layouts: 0.88 us -> 0.01 us
    all_to_all x1, starting transfers between devices: 15.3 us -> 5.75 us  [step(): lax.all_to_all(partial, both, split_axis=0, concat_axis=0, tiled=True)]
    all_to_all x1, waiting for transfers between devices: 0.01 us -> 7.19 us  [step(): lax.all_to_all(chunks, 'col', split_axis=0, concat_axis=0, tiled=True)]
    all_to_all x1, waiting for transfers between devices: 6.91 us -> 0.16 us  [step(): lax.all_to_all(partial, both, split_axis=0, concat_axis=0, tiled=True)]
    ppermute x2 -> x0, starting transfers between devices: 6.42 us -> none  [the longest x1 3.29 us: step(): bot = lax.ppermute(latent[:, :2 * WIDTH], both, down)]
    all_to_all x0 -> x1, starting transfers between devices: none -> 6.36 us  [step(): rim = lax.all_to_all(edges, 'row', split_axis=0, concat_axis=0, tiled=True)]
    pallas_call x1, Pallas kernels: 27.8 us -> 22.8 us  [step(): pl.pallas_call(main_kernel, out_shape=jax.ShapeDtypeStruct((TILE, TILE, C...]
    all_to_all x1, starting transfers between devices: 4.11 us -> 7.75 us  [step(): lax.all_to_all(chunks, 'col', split_axis=0, concat_axis=0, tiled=True)]
    pallas_call x3 -> x5, Pallas kernels: 14.6 us -> 17.9 us  [the longest x2 9.51 us: step(): pl.pallas_call(prepare_kernel, out_shape=jax.ShapeDtypeStruct((16, CH //...]
  transfers between devices with their start and end apart: 4 -> 3, of which waited for: 2 -> 3; matrix products, arithmetic and copies ran while one was open for 0% -> 0% of each run, Pallas kernels for 14% -> 18%
where the time goes in v2:
time: 72.1 us; the launch traced here: 71.6 us
  Pallas kernels  40.6 us (56%)
  starting transfers between devices  19.9 us (28%)
  waiting for transfers between devices  10.3 us (14%)
  other arithmetic  0.79 us (1%)
    pallas_call x1, Pallas kernels, step(): pl.pallas_call(main_kernel, out_shape=jax.ShapeDtypeStruct((TILE, TILE, C...  22.8 us
    pallas_call x2, Pallas kernels, step(): pl.pallas_call(prepare_kernel, out_shape=jax.ShapeDtypeStruct((16, CH //...  9.51 us
    all_to_all x1, starting transfers between devices, step(): lax.all_to_all(chunks, 'col', split_axis=0, concat_axis=0, tiled=True)  7.75 us
    all_to_all x1, waiting for transfers between devices, step(): lax.all_to_all(chunks, 'col', split_axis=0, concat_axis=0, tiled=True)  7.19 us
    all_to_all x1, starting transfers between devices, step(): rim = lax.all_to_all(edges, 'row', split_axis=0, concat_axis=0, tiled=True)  6.36 us
    all_to_all x1, starting transfers between devices, step(): lax.all_to_all(partial, both, split_axis=0, concat_axis=0, tiled=True)  5.75 us
    pallas_call x1, Pallas kernels, step(): pl.pallas_call(inner_kernel, out_shape=jax.ShapeDtypeStruct((2, 8, CH), F...  3.66 us
    all_to_all x1, waiting for transfers between devices, step(): rim = lax.all_to_all(edges, 'row', split_axis=0, concat_axis=0, tiled=True)  2.96 us
  transfers between devices with their start and end apart: 3, of which 3 were waited for; matrix products, arithmetic and copies ran while one was open for 0% of the time, Pallas kernels for 18%

profile of v2, /device:TPU:1, one launch (start us, length us, event | category | flops | bytes accessed | tf_op | source)
XLA Modules:
  0.0 71.6 jit_solution(16670477912591089952)
XLA Ops:
  0.0 2.0 %pack.1 = bf16[16,64,128]{2,1,0:T(8,128)(2,1)} custom-call(bf16[16,4096]{1,0:T(8,128)(2,1)} %own_hbm.1), custom_call_target="tpu_custom_call" | custom-call | tf_op jit(solution)/shard_map/pack/pallas_call | solution.py:388
  2.0 7.8 %all-to-all-start = ((bf16[16,64,128]{2,1,0:T(8,128)(2,1)}), bf16[16,64,128]{2,1,0:T(8,128)(2,1)S(1)}, u32[]{:S(2)}, u32[]{:S(2)}) async-start(bf16[16,64,128]{2,1,0:T(8,128)(2,1)} %pack.1), calls=%async_computation | async-start | bytes 524288 | tf_op jit(solution)/shard_map/all_to_all | solution.py:401
  9.8 7.2 %all-to-all-done = bf16[16,64,128]{2,1,0:T(8,128)(2,1)S(1)} async-done(((bf16[16,64,128]{2,1,0:T(8,128)(2,1)}), bf16[16,64,128]{2,1,0:T(8,128)(2,1)S(1)}, u32[]{:S(2)}, u32[]{:S(2)}) %all-to-all-start) | async-done | bytes 262176 | tf_op jit(solution)/shard_map/all_to_all | solution.py:401
  17.0 0.7 broadcast_select_fusion
  17.7 6.4 %all-to-all-start.1 = ((bf16[8,32,128]{2,1,0:T(8,128)(2,1)}), bf16[8,32,128]{2,1,0:T(8,128)(2,1)S(1)}, u32[]{:S(2)}, u32[]{:S(2)}) async-start(bf16[8,32,128]{2,1,0:T(8,128)(2,1)} %broadcast_select_fusion), calls=%async_computation.1 | async-start | bytes 131072 | tf_op jit(solution)/shard_map/all_to_all | solution.py:405
  24.0 0.1 pad_add_fusion.place
  24.1 3.7 %inner.1.sums = f32[2,8,512]{2,1,0:T(8,128)S(1)} custom-call(bf16[1024,128]{1,0:T(8,128)(2,1)S(1)} %bitcast.10, bf16[144,512]{1,0:T(8,128)(2,1)} %bitcast.15, f32[1,512]{1,0:T(1,128)} %bitcast.18), custom_call_target="tpu_custom_call" | custom-call | tf_op jit(solution)/shard_map/inner/pallas_call | solution.py:406
  27.8 3.0 %all-to-all-done.1.rim = bf16[8,32,128]{2,1,0:T(8,128)(2,1)S(1)} async-done(((bf16[8,32,128]{2,1,0:T(8,128)(2,1)}), bf16[8,32,128]{2,1,0:T(8,128)(2,1)S(1)}, u32[]{:S(2)}, u32[]{:S(2)}) %all-to-all-start.1) | async-done | bytes 65568 | tf_op jit(solution)/shard_map/all_to_all | solution.py:405
  30.7 2.7 %outer.1 = f32[128,1,128]{2,1,0:T(1,128)} custom-call(s32[2]{0:T(128)S(1)} %pad_add_fusion.place, bf16[1024,128]{1,0:T(8,128)(2,1)S(1)} %bitcast.11, bf16[8,32,128]{2,1,0:T(8,128)(2,1)S(1)} %all-to-all-done.1.rim, f32[2,8,512]{2,1,0:T(8,128)S(1)} %inner.1.sums, bf16[144,512]{1,0:T(8,128)(2,1)} %bitcast.16, f32[1,512]{1,0:T(1,128)} %bitcast.19), custom_call_target="tpu_custom_call" | custom-call | tf_op jit(solution)/shard_map/outer/pallas_call | solution.py:417
  33.4 5.8 %all-to-all-start.2 = ((f32[128,1,128]{2,1,0:T(1,128)}), f32[128,1,128]{2,1,0:T(1,128)S(1)}, u32[]{:S(2)}, u32[]{:S(2)}) async-start(f32[128,1,128]{2,1,0:T(1,128)} %outer.1), calls=%async_computation.2 | async-start | bytes 131072 | tf_op jit(solution)/shard_map/all_to_all | solution.py:426
  39.2 4.8 %shard_map.74.high_hbm = bf16[16,256,512]{2,1,0:T(8,128)(2,1)} custom-call(bf16[3,3,512,512]{3,2,1,0:T(8,128)(2,1)} %bitcast.13), custom_call_target="tpu_custom_call" | custom-call | tf_op jit(solution)/shard_map/pallas_call | solution.py:431
  44.0 4.7 %shard_map.73.low_hbm = bf16[16,256,512]{2,1,0:T(8,128)(2,1)} custom-call(bf16[3,3,512,512]{3,2,1,0:T(8,128)(2,1)} %bitcast.14), custom_call_target="tpu_custom_call" | custom-call | tf_op jit(solution)/shard_map/pallas_call | solution.py:431
  48.7 0.2 all-to-all-done.2.stats
  48.9 22.8 %main.1 = bf16[64,64,512]{2,1,0:T(8,128)(2,1)} custom-call(s32[2]{0:T(128)S(1)} %pad_add_fusion.place, bf16[1024,128]{1,0:T(8,128)(2,1)S(1)} %bitcast.12, bf16[8,32,128]{2,1,0:T(8,128)(2,1)S(1)} %all-to-all-done.1.rim, f32[128,1,128]{2,1,0:T(1,128)S(1)} %all-to-all-done.2.stats, bf16[144,512]{1,0:T(8,128)(2,1)} %bitcast.17, f32[1,512]{1,0:T(1,128)} %bitcast.20, ...), custom_call_target="tpu_custom_call" | custom-call | tf_op jit(solution)/shard_map/main/pallas_call | solution.py:442
  (2 shorter events, 0.0 us)
Async XLA Ops:
  2.0 14.9 %all-to-all-start = ((bf16[16,64,128]{2,1,0:T(8,128)(2,1)}), bf16[16,64,128]{2,1,0:T(8,128)(2,1)S(1)}, u32[]{:S(2)}, u32[]{:S(2)}) async-start(bf16[16,64,128]{2,1,0:T(8,128)(2,1)} %pack.1), calls=%async_computation | async-start | bytes 524288 | tf_op jit(solution)/shard_map/all_to_all | solution.py:401
  17.7 13.1 %all-to-all-start.1 = ((bf16[8,32,128]{2,1,0:T(8,128)(2,1)}), bf16[8,32,128]{2,1,0:T(8,128)(2,1)S(1)}, u32[]{:S(2)}, u32[]{:S(2)}) async-start(bf16[8,32,128]{2,1,0:T(8,128)(2,1)} %broadcast_select_fusion), calls=%async_computation.1 | async-start | bytes 131072 | tf_op jit(solution)/shard_map/all_to_all | solution.py:405
  33.4 15.4 %all-to-all-start.2 = ((f32[128,1,128]{2,1,0:T(1,128)}), f32[128,1,128]{2,1,0:T(1,128)S(1)}, u32[]{:S(2)}, u32[]{:S(2)}) async-start(f32[128,1,128]{2,1,0:T(1,128)} %outer.1), calls=%async_computation.2 | async-start | bytes 131072 | tf_op jit(solution)/shard_map/all_to_all | solution.py:426

commit v3 on v2

--- a/solution.py
+++ b/solution.py
@@ -50,15 +50,13 @@
     return copies
 
 
-def pack_kernel(own_hbm, out, rows, own, sems):
-    copies = start_copies((own_hbm,), (own,), sems)
+def pack_kernel(own, out, rows):
     k = lax.broadcasted_iota(jnp.int32, (384, 256), 0)
     n = lax.broadcasted_iota(jnp.int32, (384, 256), 1)
     lane = n % 128
     column = 64 * (n // 128) + 4 * (lane % 16) + lane // 16 + 126
     pick = jnp.where(k == column, 1.0, 0.0).astype(BF16)
     zero = jnp.zeros((64, 128), BF16)
-    copies[0].wait()
     for r in range(OWN):
         rows[16 * r : 16 * r + 16] = own[:, WIDTH * r : WIDTH * (r + 1)]
     for t in range(8):
@@ -75,8 +73,14 @@
     return total + jnp.sum(value, axis=0), squares + jnp.sum(value * value, axis=0)
 
 
-def inner_kernel(recv, weight_hbm, bias_hbm, sums, pairs, weight, bias, sems):
-    copies = start_copies((weight_hbm, bias_hbm), (weight, bias), sems)
+def inner_kernel(
+    recv, weight_hbm, bias_hbm, gain_hbm, shift_hbm, mid_bias_hbm, sums, weight, vectors, pairs, sems
+):
+    copies = start_copies(
+        (weight_hbm, bias_hbm, gain_hbm, shift_hbm, mid_bias_hbm),
+        (weight, *(vectors.at[i : i + 1] for i in range(4))),
+        sems,
+    )
     rows = recv[...].astype(F32)
     low = lax.broadcasted_iota(jnp.int32, (16 * (TILE - 1), 128), 1) < 64
     for b in range(3):
@@ -85,10 +89,8 @@
         pairs[b] = jnp.where(low, even[:-16], odd[16:]).astype(BF16)
     for copy in copies:
         copy.wait()
-    taps = weight[...]
-    shift = bias[...]
-
-    def accumulate(first, count, carry):
+
+    def contract(first, count):
         patches = [
             jnp.concatenate(
                 [
@@ -100,11 +102,21 @@
             )
             for j in range(count)
         ]
-        return add_cells(dot_tn(jnp.concatenate(patches, axis=1), taps) + shift, *carry)
+        return dot_tn(jnp.concatenate(patches, axis=1), weight[...])
+
+    def accumulate(i, carry):
+        values = [contract(GANG * i + 4 * part, 4) for part in range(GANG // 4)]
+        for value in values:
+            carry = add_cells(value, *carry)
+        return carry
 
     zero = jnp.zeros((8, CH), F32)
-    carry = lax.fori_loop(0, 7, lambda i, c: accumulate(4 * i, 4, c), (zero, zero))
-    sums[0], sums[1] = accumulate(28, 3, carry)
+    whole = 28 // GANG
+    carry = lax.fori_loop(0, whole, accumulate, (zero, zero))
+    sums[0], sums[1] = add_cells(contract(28, 3), *carry)
+
+
+GANG = 28
 
 
 def rim_rows(place, rim):
@@ -114,8 +126,7 @@
     return top, jnp.where(place[0] == N_ROW - 1, 0.0, bot)
 
 
-def outer_kernel(place, recv, rim, sums, weight_hbm, bias_hbm, out, weight, bias, sems):
-    copies = start_copies((weight_hbm, bias_hbm), (weight, bias), sems)
+def outer_kernel(place, recv, rim, sums, weight, vectors, out):
     channel = lax.broadcasted_iota(jnp.int32, (CH, 128), 0) // (CH // GROUPS)
     lane = lax.broadcasted_iota(jnp.int32, (CH, 128), 1)
     to_sum = jnp.where(channel == lane, 1.0, 0.0)
@@ -133,9 +144,11 @@
     patch = jnp.concatenate(
         [shifted[b][16 * a : 16 * a + 16] for a in range(3) for b in range(3)], axis=0
     )
-    for copy in copies:
-        copy.wait()
-    total, squares = add_cells(dot_tn(patch, weight[...]) + bias[...], sums[0], sums[1])
+    total, squares = add_cells(dot_tn(patch, weight[...]), sums[0], sums[1])
+    bias = vectors[0:1]
+    cells = TILE * TILE // 8
+    squares = squares + bias * (2.0 * total + cells * bias)
+    total = total + cells * bias
     exact = functools.partial(
         jnp.dot, precision=lax.Precision.HIGHEST, preferred_element_type=F32
     )
@@ -189,11 +202,8 @@
     recv,
     rim,
     stats,
-    taps_hbm,
-    bias_hbm,
-    gain_hbm,
-    shift_hbm,
-    mid_bias_hbm,
+    taps,
+    vectors,
     low_hbm,
     high_hbm,
     out_hbm,
@@ -207,22 +217,14 @@
     m1,
     spread,
     out,
-    taps,
-    vectors,
     points,
     in_sems,
     sems,
 ):
     loads = start_copies(
-        (taps_hbm, bias_hbm, gain_hbm, shift_hbm, mid_bias_hbm, low_hbm, high_hbm),
-        (
-            taps,
-            *(vectors.at[i : i + 1] for i in range(4)),
-            points.at[:, : CH // 2],
-            points.at[:, CH // 2 :],
-        ),
-        in_sems,
-    )
+        (low_hbm, high_hbm), (points.at[:, : CH // 2], points.at[:, CH // 2 :]), in_sems
+    )
+
     v_slots, m_slots = (v0, v1), (m0, m1)
 
     def place_rows(at, rows):
@@ -235,8 +237,6 @@
     for r in range(0, 16 * TILE, 64):
         place_rows(32 + r, recv[r : r + 64].astype(F32))
     place_rows(32 + 16 * TILE, bot)
-    for load in loads[:-2]:
-        load.wait()
     scale, offset = affine(stats, vectors[0:1], vectors[1:2], vectors[2:3])
     cell = lax.broadcasted_iota(jnp.int32, (16, CH), 0)
     hide_low = jnp.logical_and(cell == 0, place[1] == 0)
@@ -257,9 +257,9 @@
                     [lat[b, pl.ds(at + 16 * a, 16)] for a in range(3) for b in range(3)], axis=0
                 )
             )
-        raw[...] = dot_tn(jnp.concatenate(patches, axis=1), taps[...])
-
-    def activate(pair, pieces=range(4)):
+        return dot_tn(jnp.concatenate(patches, axis=1), taps[...])
+
+    def activate(pair, raw, pieces=range(4)):
         for j in range(2):
             row = 2 * pair + j
             hidden = jnp.logical_or(
@@ -316,18 +316,17 @@
                 out[2 * tile + e, l] = spread[e, l].astype(BF16)
 
     for pair in range(2):
-        contract(pair)
-        activate(pair)
+        activate(pair, contract(pair))
 
     def warm(c, _):
-        contract(c + 2)
+        value = contract(c + 2)
         build(c, v0)
-        activate(c + 2)
+        activate(c + 2, value)
         return 0
 
     lax.fori_loop(0, BLOCK, warm, 0)
-    loads[-2].wait()
-    loads[-1].wait()
+    for load in loads:
+        load.wait()
     last_pair = ACT // 2 - 1
     copies = []
     for n in range(N_BLOCK):
@@ -341,14 +340,14 @@
                 g = first + k
                 pair = jnp.minimum(g + BLOCK + 2, last_pair)
                 if ahead:
-                    contract(pair)
+                    value = contract(pair)
                 for i in range(4):
                     multiply(2 * (c * TILES + k) + i // 2, this_v, this_m, i % 2)
                     if n > 0:
                         finish(g - BLOCK, last_m, (i,))
                     if ahead:
                         build(g + BLOCK, next_v, (i,))
-                        activate(pair, (i,))
+                        activate(pair, value, (i,))
             return 0
 
         lax.fori_loop(0, BLOCK // TILES, steady, 0)
@@ -359,14 +358,18 @@
         finish((N_BLOCK - 1) * BLOCK + c, m_slots[1 - N_BLOCK % 2])
         return 0
 
-    lax.fori_loop(0, BLOCK, drain, 0)
-    copies.extend(send(out, out_hbm, N_BLOCK - 1, sems))
+    for half in range(2):
+        lax.fori_loop(half * BLOCK // 2, (half + 1) * BLOCK // 2, drain, 0)
+        copies.extend(send(out, out_hbm, N_BLOCK - 1 + half, sems, half))
     for copy in copies:
         copy.wait()
 
 
-def send(out, out_hbm, n, sems):
+def send(out, out_hbm, n, sems, half=None):
     rows = slice(2 * BLOCK * n, 2 * BLOCK * (n + 1))
+    if half is not None:
+        first = 2 * BLOCK * (N_BLOCK - 1) + BLOCK * half
+        rows = slice(first, first + BLOCK)
     copies = [
         pltpu.make_async_copy(
             out.at[rows, l], out_hbm.at[rows, :, 128 * l : 128 * l + 128], sems.at[n, l]
@@ -380,49 +383,47 @@
 
 def step(latent, in_weight, in_bias, norm_gain, norm_shift, mid_weight, mid_bias):
     both = ("row", "col")
-    taps = in_weight.reshape(9 * C_LAT, CH)
-    bias = in_bias.reshape(1, CH)
     place = jnp.stack([lax.axis_index("row"), lax.axis_index("col")]).astype(jnp.int32)
-    weights = [pltpu.VMEM((9 * C_LAT, CH), BF16), pltpu.VMEM((1, CH), F32)]
     small = pltpu.CompilerParams(vmem_limit_bytes=12 * MIB)
     chunks = pl.pallas_call(
         pack_kernel,
         out_shape=jax.ShapeDtypeStruct((N_COL, 64, 128), BF16),
-        in_specs=[HBM],
+        in_specs=[VMEM],
         out_specs=VMEM,
-        scratch_shapes=[
-            pltpu.VMEM((64, WIDTH), BF16),
-            pltpu.VMEM((C_LAT, OWN * WIDTH), BF16),
-            pltpu.SemaphoreType.DMA((1,)),
-        ],
+        scratch_shapes=[pltpu.VMEM((64, WIDTH), BF16)],
         compiler_params=small,
         name="pack",
-    )(hbm(latent))
+    )(latent)
     recv = lax.all_to_all(chunks, "col", split_axis=0, concat_axis=0, tiled=True)
     recv = recv.reshape(16 * TILE, 128)
     above = lax.broadcasted_iota(jnp.int32, (N_ROW, 32, 128), 0) > place[0]
     edges = jnp.where(above, recv[None, -32:], recv[None, :32])
     rim = lax.all_to_all(edges, "row", split_axis=0, concat_axis=0, tiled=True)
-    sums = pl.pallas_call(
+    sums, taps, vectors = pl.pallas_call(
         inner_kernel,
-        out_shape=jax.ShapeDtypeStruct((2, 8, CH), F32),
-        in_specs=[VMEM, HBM, HBM],
-        out_specs=VMEM,
-        scratch_shapes=[pltpu.VMEM((3, 16 * (TILE - 1), 128), BF16)]
-        + weights
-        + [pltpu.SemaphoreType.DMA((2,))],
+        out_shape=[
+            jax.ShapeDtypeStruct((2, 8, CH), F32),
+            jax.ShapeDtypeStruct((9 * C_LAT, CH), BF16),
+            jax.ShapeDtypeStruct((4, CH), F32),
+        ],
+        in_specs=[VMEM] + [HBM] * 5,
+        out_specs=[VMEM] * 3,
+        scratch_shapes=[pltpu.VMEM((3, 16 * (TILE - 1), 128), BF16), pltpu.SemaphoreType.DMA((5,))],
         compiler_params=small,
         name="inner",
-    )(recv, hbm(taps), hbm(bias))
+    )(
+        recv,
+        hbm(in_weight.reshape(9 * C_LAT, CH)),
+        *(hbm(v.reshape(1, CH)) for v in (in_bias, norm_gain, norm_shift, mid_bias)),
+    )
     partial = pl.pallas_call(
         outer_kernel,
         out_shape=jax.ShapeDtypeStruct((N_DEV, 1, 128), F32),
-        in_specs=[SMEM, VMEM, VMEM, VMEM, HBM, HBM],
+        in_specs=[SMEM] + [VMEM] * 5,
         out_specs=VMEM,
-        scratch_shapes=weights + [pltpu.SemaphoreType.DMA((2,))],
         compiler_params=small,
         name="outer",
-    )(place, recv, rim, sums, hbm(taps), hbm(bias))
+    )(place, recv, rim, sums, taps, vectors)
     stats = lax.all_to_all(partial, both, split_axis=0, concat_axis=0, tiled=True)
     weight = hbm(jnp.transpose(mid_weight, (1, 2, 0, 3)))
     points = []
@@ -431,18 +432,18 @@
             pl.pallas_call(
                 prepare_kernel,
                 out_shape=jax.ShapeDtypeStruct((16, CH // 2, CH), BF16),
-                grid=(4,),
+                grid=(2,),
                 in_specs=[
-                    pl.BlockSpec((3, 3, CH // 8, CH), lambda i, part=part: (0, 0, i + 4 * part, 0))
+                    pl.BlockSpec((3, 3, CH // 4, CH), lambda i, part=part: (0, 0, i + 2 * part, 0))
                 ],
-                out_specs=pl.BlockSpec((16, CH // 8, CH), lambda i: (0, i, 0)),
+                out_specs=pl.BlockSpec((16, CH // 4, CH), lambda i: (0, i, 0)),
                 compiler_params=pltpu.CompilerParams(vmem_limit_bytes=60 * MIB),
             )(weight)
         )
     return pl.pallas_call(
         main_kernel,
         out_shape=jax.ShapeDtypeStruct((TILE, TILE, CH), BF16),
-        in_specs=[SMEM, VMEM, VMEM, VMEM] + [HBM] * 7,
+        in_specs=[SMEM] + [VMEM] * 5 + [HBM] * 2,
         out_specs=HBM,
         scratch_shapes=[
             pltpu.VMEM((3, LAT * 16, 128), BF16),
@@ -455,11 +456,9 @@
             pltpu.VMEM((16, 4, M_ROWS, 128), F32),
             pltpu.VMEM((2, 4, TILE, 128), F32),
             pltpu.VMEM((TILE, 4, TILE, 128), BF16),
-            pltpu.VMEM((9 * C_LAT, CH), BF16),
-            pltpu.VMEM((4, CH), F32),
             pltpu.VMEM((16, CH, CH), BF16),
-            pltpu.SemaphoreType.DMA((7,)),
-            pltpu.SemaphoreType.DMA((N_BLOCK, 4)),
+            pltpu.SemaphoreType.DMA((2,)),
+            pltpu.SemaphoreType.DMA((N_BLOCK + 1, 4)),
         ],
         compiler_params=pltpu.CompilerParams(vmem_limit_bytes=52 * MIB),
         name="main",
@@ -468,11 +467,8 @@
         recv,
         rim,
         stats,
-        hbm(taps),
-        hbm(bias),
-        hbm(norm_gain.reshape(1, CH)),
-        hbm(norm_shift.reshape(1, CH)),
-        hbm(mid_bias.reshape(1, CH)),
+        taps,
+        vectors,
         hbm(points[0]),
         hbm(points[1]),
     )

time: 72.1 us -> 70 us (0.971)
  Pallas kernels: 40.6 us -> 34.5 us
  waiting for transfers between devices: 10.3 us -> 13.6 us
  local copies, waits for them, and re-layouts: 0.01 us -> 0.91 us
    pallas_call x2, Pallas kernels: 9.51 us -> 7.61 us  [step(): pl.pallas_call(prepare_kernel, out_shape=jax.ShapeDtypeStruct((16, CH //...]
    all_to_all x1, waiting for transfers between devices: 0.16 us -> 2.05 us  [step(): lax.all_to_all(partial, both, split_axis=0, concat_axis=0, tiled=True)]
    all_to_all x1, waiting for transfers between devices: 2.96 us -> 4.37 us  [step(): rim = lax.all_to_all(edges, 'row', split_axis=0, concat_axis=0, tiled=True)]
    pallas_call x1, Pallas kernels: 3.66 us -> 2.24 us  [step(): pl.pallas_call(inner_kernel, out_shape=[jax.ShapeDtypeStruct((2, 8, CH),...]
    pallas_call x1, Pallas kernels: 22.8 us -> 21.6 us  [step(): pl.pallas_call(main_kernel, out_shape=jax.ShapeDtypeStruct((TILE, TILE, C...]
    unnamed x0 -> x2, local copies, waits for them, and re-layouts: none -> 0.9 us
    pallas_call x1, Pallas kernels: 2 us -> 1.13 us  [step(): pl.pallas_call(pack_kernel, out_shape=jax.ShapeDtypeStruct((N_COL, 64, 12...]
    pallas_call x1, Pallas kernels: 2.69 us -> 1.85 us  [step(): pl.pallas_call(outer_kernel, out_shape=jax.ShapeDtypeStruct((N_DEV, 1, 12...]
  transfers between devices with their start and end apart: 3 -> 3, of which waited for: 3 -> 3; matrix products, arithmetic and copies ran while one was open for 0% -> 0% of each run, Pallas kernels for 18% -> 14%
where the time goes in v3:
time: 70 us; the launch traced here: 69.6 us
  Pallas kernels  34.5 us (49%)
  starting transfers between devices  19.8 us (28%)
  waiting for transfers between devices  13.6 us (19%)
  local copies, waits for them, and re-layouts  0.91 us (1%)
  other arithmetic  0.79 us (1%)
    pallas_call x1, Pallas kernels, step(): pl.pallas_call(main_kernel, out_shape=jax.ShapeDtypeStruct((TILE, TILE, C...  21.6 us
    all_to_all x1, starting transfers between devices, step(): lax.all_to_all(chunks, 'col', split_axis=0, concat_axis=0, tiled=True)  7.74 us
    pallas_call x2, Pallas kernels, step(): pl.pallas_call(prepare_kernel, out_shape=jax.ShapeDtypeStruct((16, CH //...  7.61 us
    all_to_all x1, waiting for transfers between devices, step(): lax.all_to_all(chunks, 'col', split_axis=0, concat_axis=0, tiled=True)  7.19 us
    all_to_all x1, starting transfers between devices, step(): rim = lax.all_to_all(edges, 'row', split_axis=0, concat_axis=0, tiled=True)  6.36 us
    all_to_all x1, starting transfers between devices, step(): lax.all_to_all(partial, both, split_axis=0, concat_axis=0, tiled=True)  5.73 us
    all_to_all x1, waiting for transfers between devices, step(): rim = lax.all_to_all(edges, 'row', split_axis=0, concat_axis=0, tiled=True)  4.37 us
    pallas_call x1, Pallas kernels, step(): pl.pallas_call(inner_kernel, out_shape=[jax.ShapeDtypeStruct((2, 8, CH),...  2.24 us
  transfers between devices with their start and end apart: 3, of which 3 were waited for; matrix products, arithmetic and copies ran while one was open for 0% of the time, Pallas kernels for 14%

profile of v3, /device:TPU:1, one launch (start us, length us, event | category | flops | bytes accessed | tf_op | source)
XLA Modules:
  0.0 69.6 jit_solution(16818851921966809750)
XLA Ops:
  0.0 0.0 copy-start
  0.0 0.9 %copy-done = bf16[16,4096]{1,0:T(8,128)(2,1)S(1)} copy-done((bf16[16,4096]{1,0:T(8,128)(2,1)S(1)}, bf16[16,4096]{1,0:T(8,128)(2,1)}, u32[]{:S(2)}) %copy-start) | copy-done | bytes 131096
  0.9 1.1 %pack.1 = bf16[16,64,128]{2,1,0:T(8,128)(2,1)} custom-call(bf16[16,4096]{1,0:T(8,128)(2,1)S(1)} %copy-done), custom_call_target="tpu_custom_call" | custom-call | tf_op jit(solution)/shard_map/pack/pallas_call | solution.py:388
  2.0 7.7 %all-to-all-start = ((bf16[16,64,128]{2,1,0:T(8,128)(2,1)}), bf16[16,64,128]{2,1,0:T(8,128)(2,1)S(1)}, u32[]{:S(2)}, u32[]{:S(2)}) async-start(bf16[16,64,128]{2,1,0:T(8,128)(2,1)} %pack.1), calls=%async_computation | async-start | bytes 524288 | tf_op jit(solution)/shard_map/all_to_all | solution.py:397
  9.8 7.2 %all-to-all-done = bf16[16,64,128]{2,1,0:T(8,128)(2,1)S(1)} async-done(((bf16[16,64,128]{2,1,0:T(8,128)(2,1)}), bf16[16,64,128]{2,1,0:T(8,128)(2,1)S(1)}, u32[]{:S(2)}, u32[]{:S(2)}) %all-to-all-start) | async-done | bytes 262176 | tf_op jit(solution)/shard_map/all_to_all | solution.py:397
  17.0 0.7 %broadcast_select_fusion = bf16[8,32,128]{2,1,0:T(8,128)(2,1)} fusion(pred[8]{0:T(512)(128)(4,1)S(1)} %iota_compare_fusion, bf16[32,128]{1,0:T(8,128)(2,1)S(1)} %get-tuple-element.12, bf16[32,128]{1,0:T(8,128)(2,1)S(1)} %get-tuple-element.11), kind=kLoop, calls=%fused_computation | loop fusion | flops 32768 | bytes 81928 | tf_op jit(solution)/shard_map/jit(_where)/select_n | solution.py:400
  17.7 6.4 %all-to-all-start.1 = ((bf16[8,32,128]{2,1,0:T(8,128)(2,1)}), bf16[8,32,128]{2,1,0:T(8,128)(2,1)S(1)}, u32[]{:S(2)}, u32[]{:S(2)}) async-start(bf16[8,32,128]{2,1,0:T(8,128)(2,1)} %broadcast_select_fusion), calls=%async_computation.1 | async-start | bytes 131072 | tf_op jit(solution)/shard_map/all_to_all | solution.py:401
  24.0 0.1 pad_add_fusion.place
  24.1 2.2 %inner.1 = (f32[2,8,512]{2,1,0:T(8,128)S(1)}, bf16[144,512]{1,0:T(8,128)(2,1)S(1)}, f32[4,512]{1,0:T(4,128)S(1)}) custom-call(bf16[1024,128]{1,0:T(8,128)(2,1)S(1)} %bitcast.10, bf16[144,512]{1,0:T(8,128)(2,1)} %bitcast.15, f32[1,512]{1,0:T(1,128)} %bitcast.16, f32[1,512]{1,0:T(1,128)} %bitcast.17, f32[1,512]{1,0:T(1,128)} %bitcast.18, f32[1,512]{1,0:T(1,128)} %bitcast.19), custom_call_target="tpu_custom_call" | custom-call | tf_op jit(solution)/shard_map/inner/pallas_call | solution.py:402
  26.4 4.4 %all-to-all-done.1.rim = bf16[8,32,128]{2,1,0:T(8,128)(2,1)S(1)} async-done(((bf16[8,32,128]{2,1,0:T(8,128)(2,1)}), bf16[8,32,128]{2,1,0:T(8,128)(2,1)S(1)}, u32[]{:S(2)}, u32[]{:S(2)}) %all-to-all-start.1) | async-done | bytes 65568 | tf_op jit(solution)/shard_map/all_to_all | solution.py:401
  30.7 1.9 %outer.1 = f32[128,1,128]{2,1,0:T(1,128)} custom-call(s32[2]{0:T(128)S(1)} %pad_add_fusion.place, bf16[1024,128]{1,0:T(8,128)(2,1)S(1)} %bitcast.11, bf16[8,32,128]{2,1,0:T(8,128)(2,1)S(1)} %all-to-all-done.1.rim, f32[2,8,512]{2,1,0:T(8,128)S(1)} %get-tuple-element.8.sums, bf16[144,512]{1,0:T(8,128)(2,1)S(1)} %get-tuple-element.9.weight.taps, ...), custom_call_target="tpu_custom_call" | custom-call | tf_op jit(solution)/shard_map/outer/pallas_call | solution.py:419
  32.6 5.7 %all-to-all-start.2 = ((f32[128,1,128]{2,1,0:T(1,128)}), f32[128,1,128]{2,1,0:T(1,128)S(1)}, u32[]{:S(2)}, u32[]{:S(2)}) async-start(f32[128,1,128]{2,1,0:T(1,128)} %outer.1), calls=%async_computation.2 | async-start | bytes 131072 | tf_op jit(solution)/shard_map/all_to_all | solution.py:427
  38.3 3.8 %shard_map.74.high_hbm = bf16[16,256,512]{2,1,0:T(8,128)(2,1)} custom-call(bf16[3,3,512,512]{3,2,1,0:T(8,128)(2,1)} %bitcast.13), custom_call_target="tpu_custom_call" | custom-call | tf_op jit(solution)/shard_map/pallas_call | solution.py:432
  42.2 3.8 %shard_map.73.low_hbm = bf16[16,256,512]{2,1,0:T(8,128)(2,1)} custom-call(bf16[3,3,512,512]{3,2,1,0:T(8,128)(2,1)} %bitcast.14), custom_call_target="tpu_custom_call" | custom-call | tf_op jit(solution)/shard_map/pallas_call | solution.py:432
  45.9 2.1 %all-to-all-done.2.stats = f32[128,1,128]{2,1,0:T(1,128)S(1)} async-done(((f32[128,1,128]{2,1,0:T(1,128)}), f32[128,1,128]{2,1,0:T(1,128)S(1)}, u32[]{:S(2)}, u32[]{:S(2)}) %all-to-all-start.2) | async-done | bytes 65568 | tf_op jit(solution)/shard_map/all_to_all | solution.py:427
  48.0 21.6 %main.1 = bf16[64,64,512]{2,1,0:T(8,128)(2,1)} custom-call(s32[2]{0:T(128)S(1)} %pad_add_fusion.place, bf16[1024,128]{1,0:T(8,128)(2,1)S(1)} %bitcast.12, bf16[8,32,128]{2,1,0:T(8,128)(2,1)S(1)} %all-to-all-done.1.rim, f32[128,1,128]{2,1,0:T(1,128)S(1)} %all-to-all-done.2.stats, bf16[144,512]{1,0:T(8,128)(2,1)S(1)} %get-tuple-element.9.weight.taps, ...), custom_call_target="tpu_custom_call" | custom-call | tf_op jit(solution)/shard_map/main/pallas_call | solution.py:443
  (2 shorter events, 0.0 us)
Async XLA Ops:
  0.0 0.9 %copy-start = (bf16[16,4096]{1,0:T(8,128)(2,1)S(1)}, bf16[16,4096]{1,0:T(8,128)(2,1)}, u32[]{:S(2)}) copy-start(bf16[16,4096]{1,0:T(8,128)(2,1)} %own.1) | copy-start | bytes 393220
  2.0 14.9 %all-to-all-start = ((bf16[16,64,128]{2,1,0:T(8,128)(2,1)}), bf16[16,64,128]{2,1,0:T(8,128)(2,1)S(1)}, u32[]{:S(2)}, u32[]{:S(2)}) async-start(bf16[16,64,128]{2,1,0:T(8,128)(2,1)} %pack.1), calls=%async_computation | async-start | bytes 524288 | tf_op jit(solution)/shard_map/all_to_all | solution.py:397
  17.7 13.1 %all-to-all-start.1 = ((bf16[8,32,128]{2,1,0:T(8,128)(2,1)}), bf16[8,32,128]{2,1,0:T(8,128)(2,1)S(1)}, u32[]{:S(2)}, u32[]{:S(2)}) async-start(bf16[8,32,128]{2,1,0:T(8,128)(2,1)} %broadcast_select_fusion), calls=%async_computation.1 | async-start | bytes 131072 | tf_op jit(solution)/shard_map/all_to_all | solution.py:401
  32.6 15.4 %all-to-all-start.2 = ((f32[128,1,128]{2,1,0:T(1,128)}), f32[128,1,128]{2,1,0:T(1,128)S(1)}, u32[]{:S(2)}, u32[]{:S(2)}) async-start(f32[128,1,128]{2,1,0:T(1,128)} %outer.1), calls=%async_computation.2 | async-start | bytes 131072 | tf_op jit(solution)/shard_map/all_to_all | solution.py:427

commit v4 on v3

--- a/solution.py
+++ b/solution.py
@@ -304,14 +304,16 @@
                     sums = []
                     for u in range(4):
                         m = [slot[4 * u + v, l, pl.ds(base + 16 * q + 8 * h, 8)] for v in range(4)]
+                        if u == 1:
+                            m[1] = m[1] + bias
                         both, apart = m[1] + m[2], m[1] - m[2]
                         sums.append((m[0] + both, apart - m[3]))
                     for f in range(2):
                         z = [sums[u][f] for u in range(4)]
                         both, apart = z[1] + z[2], z[1] - z[2]
                         at = pl.ds(32 * h + 2 * q + f, 8, stride=4)
-                        spread[0, l, at] = z[0] + both + bias
-                        spread[1, l, at] = apart - z[3] + bias
+                        spread[0, l, at] = z[0] + both
+                        spread[1, l, at] = apart - z[3]
             for e in range(2):
                 out[2 * tile + e, l] = spread[e, l].astype(BF16)
 

time: 70 us -> 70.1 us (level)
  no operation moved by 1% of the time
where the time goes in v4:
time: 70.1 us; the launch traced here: 69.7 us
  Pallas kernels  34.5 us (49%)
  starting transfers between devices  19.8 us (28%)
  waiting for transfers between devices  13.6 us (19%)
  local copies, waits for them, and re-layouts  0.91 us (1%)
  other arithmetic  0.79 us (1%)
    pallas_call x1, Pallas kernels, step(): pl.pallas_call(main_kernel, out_shape=jax.ShapeDtypeStruct((TILE, TILE, C...  21.7 us
    all_to_all x1, starting transfers between devices, step(): lax.all_to_all(chunks, 'col', split_axis=0, concat_axis=0, tiled=True)  7.74 us
    pallas_call x2, Pallas kernels, step(): pl.pallas_call(prepare_kernel, out_shape=jax.ShapeDtypeStruct((16, CH //...  7.61 us
    all_to_all x1, waiting for transfers between devices, step(): lax.all_to_all(chunks, 'col', split_axis=0, concat_axis=0, tiled=True)  7.19 us
    all_to_all x1, starting transfers between devices, step(): rim = lax.all_to_all(edges, 'row', split_axis=0, concat_axis=0, tiled=True)  6.36 us
    all_to_all x1, starting transfers between devices, step(): lax.all_to_all(partial, both, split_axis=0, concat_axis=0, tiled=True)  5.73 us
    all_to_all x1, waiting for transfers between devices, step(): rim = lax.all_to_all(edges, 'row', split_axis=0, concat_axis=0, tiled=True)  4.37 us
    pallas_call x1, Pallas kernels, step(): pl.pallas_call(inner_kernel, out_shape=[jax.ShapeDtypeStruct((2, 8, CH),...  2.24 us
  transfers between devices with their start and end apart: 3, of which 3 were waited for; matrix products, arithmetic and copies ran while one was open for 0% of the time, Pallas kernels for 14%

profile of v4, /device:TPU:1, one launch (start us, length us, event | category | flops | bytes accessed | tf_op | source)
XLA Modules:
  0.0 69.7 jit_solution(263632982882211390)
XLA Ops:
  0.0 0.0 copy-start
  0.0 0.9 %copy-done = bf16[16,4096]{1,0:T(8,128)(2,1)S(1)} copy-done((bf16[16,4096]{1,0:T(8,128)(2,1)S(1)}, bf16[16,4096]{1,0:T(8,128)(2,1)}, u32[]{:S(2)}) %copy-start) | copy-done | bytes 131096
  0.9 1.1 %pack.1 = bf16[16,64,128]{2,1,0:T(8,128)(2,1)} custom-call(bf16[16,4096]{1,0:T(8,128)(2,1)S(1)} %copy-done), custom_call_target="tpu_custom_call" | custom-call | tf_op jit(solution)/shard_map/pack/pallas_call | solution.py:390
  2.0 7.7 %all-to-all-start = ((bf16[16,64,128]{2,1,0:T(8,128)(2,1)}), bf16[16,64,128]{2,1,0:T(8,128)(2,1)S(1)}, u32[]{:S(2)}, u32[]{:S(2)}) async-start(bf16[16,64,128]{2,1,0:T(8,128)(2,1)} %pack.1), calls=%async_computation | async-start | bytes 524288 | tf_op jit(solution)/shard_map/all_to_all | solution.py:399
  9.8 7.2 %all-to-all-done = bf16[16,64,128]{2,1,0:T(8,128)(2,1)S(1)} async-done(((bf16[16,64,128]{2,1,0:T(8,128)(2,1)}), bf16[16,64,128]{2,1,0:T(8,128)(2,1)S(1)}, u32[]{:S(2)}, u32[]{:S(2)}) %all-to-all-start) | async-done | bytes 262176 | tf_op jit(solution)/shard_map/all_to_all | solution.py:399
  17.0 0.7 %broadcast_select_fusion = bf16[8,32,128]{2,1,0:T(8,128)(2,1)} fusion(pred[8]{0:T(512)(128)(4,1)S(1)} %iota_compare_fusion, bf16[32,128]{1,0:T(8,128)(2,1)S(1)} %get-tuple-element.12, bf16[32,128]{1,0:T(8,128)(2,1)S(1)} %get-tuple-element.11), kind=kLoop, calls=%fused_computation | loop fusion | flops 32768 | bytes 81928 | tf_op jit(solution)/shard_map/jit(_where)/select_n | solution.py:402
  17.7 6.4 %all-to-all-start.1 = ((bf16[8,32,128]{2,1,0:T(8,128)(2,1)}), bf16[8,32,128]{2,1,0:T(8,128)(2,1)S(1)}, u32[]{:S(2)}, u32[]{:S(2)}) async-start(bf16[8,32,128]{2,1,0:T(8,128)(2,1)} %broadcast_select_fusion), calls=%async_computation.1 | async-start | bytes 131072 | tf_op jit(solution)/shard_map/all_to_all | solution.py:403
  24.0 0.1 pad_add_fusion.place
  24.1 2.2 %inner.1 = (f32[2,8,512]{2,1,0:T(8,128)S(1)}, bf16[144,512]{1,0:T(8,128)(2,1)S(1)}, f32[4,512]{1,0:T(4,128)S(1)}) custom-call(bf16[1024,128]{1,0:T(8,128)(2,1)S(1)} %bitcast.10, bf16[144,512]{1,0:T(8,128)(2,1)} %bitcast.15, f32[1,512]{1,0:T(1,128)} %bitcast.16, f32[1,512]{1,0:T(1,128)} %bitcast.17, f32[1,512]{1,0:T(1,128)} %bitcast.18, f32[1,512]{1,0:T(1,128)} %bitcast.19), custom_call_target="tpu_custom_call" | custom-call | tf_op jit(solution)/shard_map/inner/pallas_call | solution.py:404
  26.4 4.4 %all-to-all-done.1.rim = bf16[8,32,128]{2,1,0:T(8,128)(2,1)S(1)} async-done(((bf16[8,32,128]{2,1,0:T(8,128)(2,1)}), bf16[8,32,128]{2,1,0:T(8,128)(2,1)S(1)}, u32[]{:S(2)}, u32[]{:S(2)}) %all-to-all-start.1) | async-done | bytes 65568 | tf_op jit(solution)/shard_map/all_to_all | solution.py:403
  30.7 1.9 %outer.1 = f32[128,1,128]{2,1,0:T(1,128)} custom-call(s32[2]{0:T(128)S(1)} %pad_add_fusion.place, bf16[1024,128]{1,0:T(8,128)(2,1)S(1)} %bitcast.11, bf16[8,32,128]{2,1,0:T(8,128)(2,1)S(1)} %all-to-all-done.1.rim, f32[2,8,512]{2,1,0:T(8,128)S(1)} %get-tuple-element.8.sums, bf16[144,512]{1,0:T(8,128)(2,1)S(1)} %get-tuple-element.9.weight.taps, ...), custom_call_target="tpu_custom_call" | custom-call | tf_op jit(solution)/shard_map/outer/pallas_call | solution.py:421
  32.6 5.7 %all-to-all-start.2 = ((f32[128,1,128]{2,1,0:T(1,128)}), f32[128,1,128]{2,1,0:T(1,128)S(1)}, u32[]{:S(2)}, u32[]{:S(2)}) async-start(f32[128,1,128]{2,1,0:T(1,128)} %outer.1), calls=%async_computation.2 | async-start | bytes 131072 | tf_op jit(solution)/shard_map/all_to_all | solution.py:429
  38.3 3.8 %shard_map.74.high_hbm = bf16[16,256,512]{2,1,0:T(8,128)(2,1)} custom-call(bf16[3,3,512,512]{3,2,1,0:T(8,128)(2,1)} %bitcast.13), custom_call_target="tpu_custom_call" | custom-call | tf_op jit(solution)/shard_map/pallas_call | solution.py:434
  42.2 3.8 %shard_map.73.low_hbm = bf16[16,256,512]{2,1,0:T(8,128)(2,1)} custom-call(bf16[3,3,512,512]{3,2,1,0:T(8,128)(2,1)} %bitcast.14), custom_call_target="tpu_custom_call" | custom-call | tf_op jit(solution)/shard_map/pallas_call | solution.py:434
  45.9 2.1 %all-to-all-done.2.stats = f32[128,1,128]{2,1,0:T(1,128)S(1)} async-done(((f32[128,1,128]{2,1,0:T(1,128)}), f32[128,1,128]{2,1,0:T(1,128)S(1)}, u32[]{:S(2)}, u32[]{:S(2)}) %all-to-all-start.2) | async-done | bytes 65568 | tf_op jit(solution)/shard_map/all_to_all | solution.py:429
  48.0 21.7 %main.1 = bf16[64,64,512]{2,1,0:T(8,128)(2,1)} custom-call(s32[2]{0:T(128)S(1)} %pad_add_fusion.place, bf16[1024,128]{1,0:T(8,128)(2,1)S(1)} %bitcast.12, bf16[8,32,128]{2,1,0:T(8,128)(2,1)S(1)} %all-to-all-done.1.rim, f32[128,1,128]{2,1,0:T(1,128)S(1)} %all-to-all-done.2.stats, bf16[144,512]{1,0:T(8,128)(2,1)S(1)} %get-tuple-element.9.weight.taps, ...), custom_call_target="tpu_custom_call" | custom-call | tf_op jit(solution)/shard_map/main/pallas_call | solution.py:445
  (2 shorter events, 0.0 us)
Async XLA Ops:
  0.0 0.9 %copy-start = (bf16[16,4096]{1,0:T(8,128)(2,1)S(1)}, bf16[16,4096]{1,0:T(8,128)(2,1)}, u32[]{:S(2)}) copy-start(bf16[16,4096]{1,0:T(8,128)(2,1)} %own.1) | copy-start | bytes 393220
  2.0 14.9 %all-to-all-start = ((bf16[16,64,128]{2,1,0:T(8,128)(2,1)}), bf16[16,64,128]{2,1,0:T(8,128)(2,1)S(1)}, u32[]{:S(2)}, u32[]{:S(2)}) async-start(bf16[16,64,128]{2,1,0:T(8,128)(2,1)} %pack.1), calls=%async_computation | async-start | bytes 524288 | tf_op jit(solution)/shard_map/all_to_all | solution.py:399
  17.7 13.1 %all-to-all-start.1 = ((bf16[8,32,128]{2,1,0:T(8,128)(2,1)}), bf16[8,32,128]{2,1,0:T(8,128)(2,1)S(1)}, u32[]{:S(2)}, u32[]{:S(2)}) async-start(bf16[8,32,128]{2,1,0:T(8,128)(2,1)} %broadcast_select_fusion), calls=%async_computation.1 | async-start | bytes 131072 | tf_op jit(solution)/shard_map/all_to_all | solution.py:403
  32.6 15.4 %all-to-all-start.2 = ((f32[128,1,128]{2,1,0:T(1,128)}), f32[128,1,128]{2,1,0:T(1,128)S(1)}, u32[]{:S(2)}, u32[]{:S(2)}) async-start(f32[128,1,128]{2,1,0:T(1,128)} %outer.1), calls=%async_computation.2 | async-start | bytes 131072 | tf_op jit(solution)/shard_map/all_to_all | solution.py:429

commit v5 on v3

--- a/solution.py
+++ b/solution.py
@@ -130,7 +130,6 @@
     channel = lax.broadcasted_iota(jnp.int32, (CH, 128), 0) // (CH // GROUPS)
     lane = lax.broadcasted_iota(jnp.int32, (CH, 128), 1)
     to_sum = jnp.where(channel == lane, 1.0, 0.0)
-    to_squares = jnp.where(channel == lane - GROUPS, 1.0, 0.0)
     top, bot = rim_rows(place, rim)
     first = jnp.concatenate([top[16:], recv[0:32].astype(F32)], axis=0)
     last = jnp.concatenate([recv[16 * TILE - 32 :].astype(F32), bot[:16]], axis=0)
@@ -152,7 +151,8 @@
     exact = functools.partial(
         jnp.dot, precision=lax.Precision.HIGHEST, preferred_element_type=F32
     )
-    both = exact(total, to_sum) + exact(squares, to_squares)
+    both = exact(jnp.concatenate([total, squares], axis=0), to_sum)
+    both = both[0:8] + pltpu.roll(both[8:16], GROUPS, 1)
     out[...] = jnp.broadcast_to(jnp.sum(both, axis=0).reshape(1, 1, 128), (N_DEV, 1, 128))
 
 
@@ -164,8 +164,9 @@
     spread = functools.partial(
         jnp.dot, precision=lax.Precision.HIGHEST, preferred_element_type=F32
     )
-    mean = spread(sums, jnp.where(channel == lane, 1.0, 0.0))[0:1]
-    square = spread(sums, jnp.where(channel == lane - GROUPS, 1.0, 0.0))[0:1]
+    rows = jnp.concatenate([sums, pltpu.roll(sums, 128 - GROUPS, 1)], axis=0)
+    moments = spread(rows, jnp.where(channel == lane, 1.0, 0.0))
+    mean, square = moments[0:1], moments[8:9]
     scale = lax.rsqrt(square - mean * mean + EPSILON) * gain[...]
     return scale, (bias[...] - mean) * scale + shift[...]
 

time: 70 us -> 70 us (level)
  no operation moved by 1% of the time
where the time goes in v5:
time: 70 us; the launch traced here: 69.6 us
  Pallas kernels  34.4 us (49%)
  starting transfers between devices  19.8 us (28%)
  waiting for transfers between devices  13.6 us (19%)
  local copies, waits for them, and re-layouts  0.91 us (1%)
  other arithmetic  0.79 us (1%)
    pallas_call x1, Pallas kernels, step(): pl.pallas_call(main_kernel, out_shape=jax.ShapeDtypeStruct((TILE, TILE, C...  21.6 us
    all_to_all x1, starting transfers between devices, step(): lax.all_to_all(chunks, 'col', split_axis=0, concat_axis=0, tiled=True)  7.74 us
    pallas_call x2, Pallas kernels, step(): pl.pallas_call(prepare_kernel, out_shape=jax.ShapeDtypeStruct((16, CH //...  7.61 us
    all_to_all x1, waiting for transfers between devices, step(): lax.all_to_all(chunks, 'col', split_axis=0, concat_axis=0, tiled=True)  7.19 us
    all_to_all x1, starting transfers between devices, step(): rim = lax.all_to_all(edges, 'row', split_axis=0, concat_axis=0, tiled=True)  6.36 us
    all_to_all x1, starting transfers between devices, step(): lax.all_to_all(partial, both, split_axis=0, concat_axis=0, tiled=True)  5.73 us
    all_to_all x1, waiting for transfers between devices, step(): rim = lax.all_to_all(edges, 'row', split_axis=0, concat_axis=0, tiled=True)  4.37 us
    pallas_call x1, Pallas kernels, step(): pl.pallas_call(inner_kernel, out_shape=[jax.ShapeDtypeStruct((2, 8, CH),...  2.24 us
  transfers between devices with their start and end apart: 3, of which 3 were waited for; matrix products, arithmetic and copies ran while one was open for 0% of the time, Pallas kernels for 14%

profile of v5, /device:TPU:1, one launch (start us, length us, event | category | flops | bytes accessed | tf_op | source)
XLA Modules:
  0.0 69.6 jit_solution(16573434411516489587)
XLA Ops:
  0.0 0.0 copy-start
  0.0 0.9 %copy-done = bf16[16,4096]{1,0:T(8,128)(2,1)S(1)} copy-done((bf16[16,4096]{1,0:T(8,128)(2,1)S(1)}, bf16[16,4096]{1,0:T(8,128)(2,1)}, u32[]{:S(2)}) %copy-start) | copy-done | bytes 131096
  0.9 1.1 %pack.1 = bf16[16,64,128]{2,1,0:T(8,128)(2,1)} custom-call(bf16[16,4096]{1,0:T(8,128)(2,1)S(1)} %copy-done), custom_call_target="tpu_custom_call" | custom-call | tf_op jit(solution)/shard_map/pack/pallas_call | solution.py:389
  2.0 7.7 %all-to-all-start = ((bf16[16,64,128]{2,1,0:T(8,128)(2,1)}), bf16[16,64,128]{2,1,0:T(8,128)(2,1)S(1)}, u32[]{:S(2)}, u32[]{:S(2)}) async-start(bf16[16,64,128]{2,1,0:T(8,128)(2,1)} %pack.1), calls=%async_computation | async-start | bytes 524288 | tf_op jit(solution)/shard_map/all_to_all | solution.py:398
  9.8 7.2 %all-to-all-done = bf16[16,64,128]{2,1,0:T(8,128)(2,1)S(1)} async-done(((bf16[16,64,128]{2,1,0:T(8,128)(2,1)}), bf16[16,64,128]{2,1,0:T(8,128)(2,1)S(1)}, u32[]{:S(2)}, u32[]{:S(2)}) %all-to-all-start) | async-done | bytes 262176 | tf_op jit(solution)/shard_map/all_to_all | solution.py:398
  17.0 0.7 %broadcast_select_fusion = bf16[8,32,128]{2,1,0:T(8,128)(2,1)} fusion(pred[8]{0:T(512)(128)(4,1)S(1)} %iota_compare_fusion, bf16[32,128]{1,0:T(8,128)(2,1)S(1)} %get-tuple-element.12, bf16[32,128]{1,0:T(8,128)(2,1)S(1)} %get-tuple-element.11), kind=kLoop, calls=%fused_computation | loop fusion | flops 32768 | bytes 81928 | tf_op jit(solution)/shard_map/jit(_where)/select_n | solution.py:401
  17.7 6.4 %all-to-all-start.1 = ((bf16[8,32,128]{2,1,0:T(8,128)(2,1)}), bf16[8,32,128]{2,1,0:T(8,128)(2,1)S(1)}, u32[]{:S(2)}, u32[]{:S(2)}) async-start(bf16[8,32,128]{2,1,0:T(8,128)(2,1)} %broadcast_select_fusion), calls=%async_computation.1 | async-start | bytes 131072 | tf_op jit(solution)/shard_map/all_to_all | solution.py:402
  24.0 0.1 pad_add_fusion.place
  24.1 2.2 %inner.1 = (f32[2,8,512]{2,1,0:T(8,128)S(1)}, bf16[144,512]{1,0:T(8,128)(2,1)S(1)}, f32[4,512]{1,0:T(4,128)S(1)}) custom-call(bf16[1024,128]{1,0:T(8,128)(2,1)S(1)} %bitcast.10, bf16[144,512]{1,0:T(8,128)(2,1)} %bitcast.15, f32[1,512]{1,0:T(1,128)} %bitcast.16, f32[1,512]{1,0:T(1,128)} %bitcast.17, f32[1,512]{1,0:T(1,128)} %bitcast.18, f32[1,512]{1,0:T(1,128)} %bitcast.19), custom_call_target="tpu_custom_call" | custom-call | tf_op jit(solution)/shard_map/inner/pallas_call | solution.py:403
  26.4 4.4 %all-to-all-done.1.rim = bf16[8,32,128]{2,1,0:T(8,128)(2,1)S(1)} async-done(((bf16[8,32,128]{2,1,0:T(8,128)(2,1)}), bf16[8,32,128]{2,1,0:T(8,128)(2,1)S(1)}, u32[]{:S(2)}, u32[]{:S(2)}) %all-to-all-start.1) | async-done | bytes 65568 | tf_op jit(solution)/shard_map/all_to_all | solution.py:402
  30.7 1.8 %outer.1 = f32[128,1,128]{2,1,0:T(1,128)} custom-call(s32[2]{0:T(128)S(1)} %pad_add_fusion.place, bf16[1024,128]{1,0:T(8,128)(2,1)S(1)} %bitcast.11, bf16[8,32,128]{2,1,0:T(8,128)(2,1)S(1)} %all-to-all-done.1.rim, f32[2,8,512]{2,1,0:T(8,128)S(1)} %get-tuple-element.8.sums, bf16[144,512]{1,0:T(8,128)(2,1)S(1)} %get-tuple-element.9.weight.taps, ...), custom_call_target="tpu_custom_call" | custom-call | tf_op jit(solution)/shard_map/outer/pallas_call | solution.py:420
  32.5 5.7 %all-to-all-start.2 = ((f32[128,1,128]{2,1,0:T(1,128)}), f32[128,1,128]{2,1,0:T(1,128)S(1)}, u32[]{:S(2)}, u32[]{:S(2)}) async-start(f32[128,1,128]{2,1,0:T(1,128)} %outer.1), calls=%async_computation.2 | async-start | bytes 131072 | tf_op jit(solution)/shard_map/all_to_all | solution.py:428
  38.3 3.8 %shard_map.74.high_hbm = bf16[16,256,512]{2,1,0:T(8,128)(2,1)} custom-call(bf16[3,3,512,512]{3,2,1,0:T(8,128)(2,1)} %bitcast.13), custom_call_target="tpu_custom_call" | custom-call | tf_op jit(solution)/shard_map/pallas_call | solution.py:433
  42.1 3.8 %shard_map.73.low_hbm = bf16[16,256,512]{2,1,0:T(8,128)(2,1)} custom-call(bf16[3,3,512,512]{3,2,1,0:T(8,128)(2,1)} %bitcast.14), custom_call_target="tpu_custom_call" | custom-call | tf_op jit(solution)/shard_map/pallas_call | solution.py:433
  45.9 2.1 %all-to-all-done.2.stats = f32[128,1,128]{2,1,0:T(1,128)S(1)} async-done(((f32[128,1,128]{2,1,0:T(1,128)}), f32[128,1,128]{2,1,0:T(1,128)S(1)}, u32[]{:S(2)}, u32[]{:S(2)}) %all-to-all-start.2) | async-done | bytes 65568 | tf_op jit(solution)/shard_map/all_to_all | solution.py:428
  47.9 21.6 %main.1 = bf16[64,64,512]{2,1,0:T(8,128)(2,1)} custom-call(s32[2]{0:T(128)S(1)} %pad_add_fusion.place, bf16[1024,128]{1,0:T(8,128)(2,1)S(1)} %bitcast.12, bf16[8,32,128]{2,1,0:T(8,128)(2,1)S(1)} %all-to-all-done.1.rim, f32[128,1,128]{2,1,0:T(1,128)S(1)} %all-to-all-done.2.stats, bf16[144,512]{1,0:T(8,128)(2,1)S(1)} %get-tuple-element.9.weight.taps, ...), custom_call_target="tpu_custom_call" | custom-call | tf_op jit(solution)/shard_map/main/pallas_call | solution.py:444
  (2 shorter events, 0.0 us)
Async XLA Ops:
  0.0 0.9 %copy-start = (bf16[16,4096]{1,0:T(8,128)(2,1)S(1)}, bf16[16,4096]{1,0:T(8,128)(2,1)}, u32[]{:S(2)}) copy-start(bf16[16,4096]{1,0:T(8,128)(2,1)} %own.1) | copy-start | bytes 393220
  2.0 14.9 %all-to-all-start = ((bf16[16,64,128]{2,1,0:T(8,128)(2,1)}), bf16[16,64,128]{2,1,0:T(8,128)(2,1)S(1)}, u32[]{:S(2)}, u32[]{:S(2)}) async-start(bf16[16,64,128]{2,1,0:T(8,128)(2,1)} %pack.1), calls=%async_computation | async-start | bytes 524288 | tf_op jit(solution)/shard_map/all_to_all | solution.py:398
  17.7 13.1 %all-to-all-start.1 = ((bf16[8,32,128]{2,1,0:T(8,128)(2,1)}), bf16[8,32,128]{2,1,0:T(8,128)(2,1)S(1)}, u32[]{:S(2)}, u32[]{:S(2)}) async-start(bf16[8,32,128]{2,1,0:T(8,128)(2,1)} %broadcast_select_fusion), calls=%async_computation.1 | async-start | bytes 131072 | tf_op jit(solution)/shard_map/all_to_all | solution.py:402
  32.5 15.4 %all-to-all-start.2 = ((f32[128,1,128]{2,1,0:T(1,128)}), f32[128,1,128]{2,1,0:T(1,128)S(1)}, u32[]{:S(2)}, u32[]{:S(2)}) async-start(f32[128,1,128]{2,1,0:T(1,128)} %outer.1), calls=%async_computation.2 | async-start | bytes 131072 | tf_op jit(solution)/shard_map/all_to_all | solution.py:428
